TPU v7x, 256 devices: a whole 4x4x8 slice. The times are simulated.
256 devices in a mesh: tok: 16 (over y, x), ch: 16 (over z, core).
Axes of the slice: x: 4, y: 4, z: 8, core: 2. Of those that a mesh axis runs over, the one named last changes fastest.
Arguments:
- tokens: bfloat16 [256, 16384], P('tok', 'ch'), may hold values from -64 to 64
- probe: int32 [256, 16384], P('tok', 'ch'), may hold values from 0 to 1
- signs: int32 [16384], P('ch'), may hold values from 0 to 1
- gate_weight: bfloat16 [16384, 26624], P('ch', 'tok'), may hold values from -0.046875 to 0.046875
- up_weight: bfloat16 [16384, 26624], P('ch', 'tok'), may hold values from -0.046875 to 0.046875
- down_weight: bfloat16 [26624, 16384], P('tok', 'ch'), may hold values from -0.0390625 to 0.0390625
Outputs:
- rotated_product: float32 [256, 16384], P('tok', 'ch')
- diagonal_estimate: float32 [16384], P('ch')
All inputs are finite; a program needn't handle non-finite values.
Results may differ from a plain program's by a relative error of at most 0.004.
Values may be sent and summed in bfloat16 or wider, within the bound.
No kernel may reach another device: no remote copies, remote signals or barrier semaphores. Data moves between devices by JAX's collectives and lax.ppermute only.
A program may use at most 128 MiB of HBM per device.

v0:
```python
import math

import jax
import jax.numpy as jnp
from jax import lax
from jax.sharding import PartitionSpec as P

D = 16384


def partner_2(value, axis, stride):
    mask = 2**stride
    pairs = [(source, source ^ mask) for source in range(lax.axis_size(axis))]
    return lax.ppermute(value, axis, pairs)


def sign_table(length):
    indices = jnp.arange(length, dtype=jnp.int32)
    parity = jnp.zeros((length, length), jnp.int32)
    for bit_pos in range(length.bit_length() - 1):
        parity = parity + (indices[:, None] >> bit_pos & 1) * (indices[None, :] >> bit_pos & 1)
    return jnp.where(parity % 2 == 0, 1.0, -1.0).astype(jnp.float32)


def cross_pairs(values):
    my_index = lax.axis_index("ch")
    for bit_pos in range(lax.axis_size("ch").bit_length() - 1):
        partner = partner_2(values, "ch", bit_pos)
        upper_half = my_index >> bit_pos & 1 == 1
        values = jnp.where(upper_half, partner - values, values + partner)
    return values


def cross_section(values):
    return cross_pairs(values)


def grad_product(gate_piece, up_piece, gate_weight, up_weight):
    contract = (((1,), (1,)), ((), ()))
    first_term = lax.dot_general(
        gate_piece, gate_weight, contract, preferred_element_type=jnp.float32
    )
    return first_term + lax.dot_general(
        up_piece, up_weight, contract, preferred_element_type=jnp.float32
    )


def on_device(tokens, probe, signs, gate_weight, up_weight, down_weight):
    tok_rows, channels = tokens.shape
    total_rows = tok_rows * lax.axis_size("tok")
    root_scale = 1.0 / math.sqrt(D)
    hadamard = sign_table(channels)
    probe_signs = (2 * probe - 1).astype(jnp.float32)
    channel_signs = (2 * signs - 1).astype(jnp.float32)
    start_local = jnp.dot(
        (probe_signs * channel_signs[None, :]).astype(jnp.bfloat16),
        hadamard.astype(jnp.bfloat16),
        preferred_element_type=jnp.float32,
    )
    tangent = (cross_section(start_local) * root_scale).astype(jnp.bfloat16)
    all_tokens, all_tangent = (
        lax.all_gather(tokens, "tok", axis=0, tiled=True),
        lax.all_gather(tangent, "tok", axis=0, tiled=True),
    )
    inputs = jnp.stack([all_tokens, all_tangent], axis=1)
    gate_part = jnp.einsum("rsd,df->rsf", inputs, gate_weight, preferred_element_type=jnp.float32)
    up_part = jnp.einsum("rsd,df->rsf", inputs, up_weight, preferred_element_type=jnp.float32)
    summed = lax.psum_scatter(
        jnp.stack([gate_part, up_part], axis=2), "ch", scatter_dimension=0, tiled=True
    )
    gate_pre = summed[:, 0, 0]
    up_pre = summed[:, 0, 1]
    gate_tan = summed[:, 1, 0]
    up_tan = summed[:, 1, 1]
    sigmoid_gate = jax.nn.sigmoid(gate_pre)
    activated = gate_pre * sigmoid_gate
    slope_term = sigmoid_gate * (1.0 + gate_pre * (1.0 - sigmoid_gate))
    hidden_tan = (slope_term * gate_tan * up_pre + activated * up_tan).astype(jnp.bfloat16)
    out_part = jnp.dot(
        lax.all_gather(hidden_tan, "ch", axis=0, tiled=True),
        down_weight,
        preferred_element_type=jnp.float32,
    )
    out_tangent = lax.psum(out_part, "tok").astype(jnp.bfloat16)
    piece = out_tangent
    back_hidden = lax.psum_scatter(
        lax.dot_general(
            piece, down_weight, (((1,), (1,)), ((), ())), preferred_element_type=jnp.float32
        ),
        "ch",
        scatter_dimension=0,
        tiled=True,
    )
    back_gate = (back_hidden * up_pre * slope_term).astype(jnp.bfloat16)
    back_up = (back_hidden * activated).astype(jnp.bfloat16)
    stacked = jnp.stack([back_gate, back_up], axis=1)
    piece = lax.all_gather(stacked, "ch", axis=0, tiled=True)
    in_part = grad_product(piece[:, 0], piece[:, 1], gate_weight, up_weight)
    back_tokens = lax.psum_scatter(in_part, "tok", scatter_dimension=0, tiled=True)
    local_back = jnp.dot(
        back_tokens, hadamard, precision=lax.Precision.HIGHEST, preferred_element_type=jnp.float32
    )
    rotated_product = cross_section(local_back) * root_scale * channel_signs[None, :]
    token_terms = jnp.sum(probe_signs * rotated_product, axis=0)
    diagonal_estimate = lax.psum(token_terms, "tok") / total_rows
    return (rotated_product, diagonal_estimate)


def solution(mesh):
    placed = (
        P("tok", "ch"),
        P("tok", "ch"),
        P("ch"),
        P("ch", "tok"),
        P("ch", "tok"),
        P("tok", "ch"),
    )
    return jax.shard_map(
        on_device, mesh=mesh, in_specs=placed, out_specs=(P("tok", "ch"), P("ch")), check_vma=False
    )
```

profile of v0, /device:TPU:32, one launch (start us, length us, event | category | flops | bytes accessed | tf_op | source)
XLA Modules:
  0.0 515.5 jit_solution(10228923519675699118)
XLA Ops:
  8.1 6.5 %fusion.3 = pred[1024,1024]{1,0:T(32,128)(4,1)S(1)} fusion(s32[1024]{0:T(1024)S(1)} %get-tuple-element.6, s32[1024]{0:T(1024)S(1)} %get-tuple-element.7, s32[1024]{0:T(1024)S(1)} %get-tuple-element.8, s32[1024]{0:T(1024)S(1)} %get-tuple-element.9, s32[1024]{0:T(1024)S(1)} %get-tuple-element.10, s32[1024]{0:T(1024)S(1)} %get-tuple-element.11, ...), kind=kLoop, calls=%fused_computation.8 | loop fusion | flops 32505856 | bytes 1089536 | tf_op jit(solution)/shard_map/eq | solution.py:22
  21.2 2.5 collective-permute-done.1
  24.5 3.4 collective-permute-start.2
  30.2 6.1 %collective-permute-start.3 = (f32[16,1024]{1,0:T(8,128)S(1)}, f32[16,1024]{1,0:T(8,128)S(1)}, u32[]{:S(2)}, u32[]{:S(2)}) collective-permute-start(f32[16,1024]{1,0:T(8,128)S(1)} %add_select_fusion.4), channel_id=1, source_target_pairs={{0,8},{1,9},{2,10},{3,11},{4,12},{5,13},{6,14},{7,15},{8,0},{9,1},... | collective-permute-start | bytes 196616 | tf_op jit(solution)/shard_map/ppermute | solution.py:14
  36.3 24.4 %all_gather.12 = bf16[256,1024]{1,0:T(8,128)(2,1)S(1)} all-gather(bf16[16,1024]{1,0:T(8,128)(2,1)} %param.6), channel_id=1, replica_groups=mesh['tok'=16,'ch'=16] {'tok'}, dimensions={0}, use_global_device_ids=true | all-gather | bytes 557056 | tf_op jit(solution)/shard_map/all_gather | solution.py:62
  60.7 23.3 %all_gather.13 = bf16[256,1024]{1,0:T(8,128)(2,1)S(1)} all-gather(bf16[16,1024]{1,0:T(8,128)(2,1)S(1)} %multiply_convert_fusion.2), channel_id=1, replica_groups=mesh['tok'=16,'ch'=16] {'tok'}, dimensions={0}, use_global_device_ids=true | all-gather | bytes 557056 | tf_op jit(solution)/shard_map/all_gather | solution.py:63
  84.0 4.0 fusion.11
  90.1 3.3 pad_maximum_fusion
  93.4 60.3 %reduce-scatter.4.cloned.1.call-done = f32[16,2,2,1664]{3,0,1,2:T(8,128)} async-done(((f32[256,2,2,1664]{3,0,1,2:T(8,128)}), f32[16,2,2,1664]{3,0,1,2:T(8,128)}) %reduce-scatter.4.cloned.1.call-update) | async-done | bytes 426000 | tf_op jit(solution)/shard_map/reduce_scatter | solution.py:68
  154.8 20.4 %all_gather.14 = bf16[256,1664]{1,0:T(8,128)(2,1)S(1)} all-gather(bf16[16,1664]{1,0:T(8,128)(2,1)S(1)} %fusion.24), channel_id=1, replica_groups=mesh['tok'=16,'ch'=16] {'ch'}, dimensions={0}, use_global_device_ids=true | all-gather | bytes 905216 | tf_op jit(solution)/shard_map/all_gather | solution.py:80
  175.3 4.1 fusion.41
  179.4 88.3 %all-reduce.1 = bf16[256,1024]{1,0:T(8,128)(2,1)} all-reduce(f32[256,1024]{1,0:T(8,128)} %fusion.41), channel_id=1, replica_groups=mesh['tok'=16,'ch'=16] {'tok'}, use_global_device_ids=true, to_apply=%region_1.2 | all-reduce | flops 262144 | bytes 1572864 | tf_op jit(solution)/shard_map/psum | solution.py:84
  267.7 4.5 fusion.42
  272.3 49.8 %reduce-scatter.6.cloned.1.call-done = f32[16,1664]{1,0:T(8,128)} async-done(((f32[256,1664]{1,0:T(8,128)}), f32[16,1664]{1,0:T(8,128)}) %reduce-scatter.6.cloned.1.call-update) | async-done | bytes 106512 | tf_op jit(solution)/shard_map/reduce_scatter | solution.py:86
  324.1 40.5 %all-gather.2.cloned.1.call-done = bf16[256,2,1664]{2,0,1:T(8,128)(2,1)} async-done(((bf16[16,2,1664]{2,0,1:T(8,128)(2,1)}), bf16[256,2,1664]{2,0,1:T(8,128)(2,1)}) %all-gather.2.cloned.1.call-update) | async-done | bytes 1703952 | tf_op jit(solution)/shard_map/all_gather | solution.py:97
  364.6 2.4 fusion.19
  369.5 77.1 %reduce-scatter.8.cloned.1.call-done = f32[16,1024]{1,0:T(8,128)} async-done(((f32[256,1024]{1,0:T(8,128)}), f32[16,1024]{1,0:T(8,128)}) %reduce-scatter.8.cloned.1.call-update) | async-done | bytes 65552 | tf_op jit(solution)/shard_map/reduce_scatter | solution.py:99
  446.6 3.6 fusion
  452.0 3.8 collective-permute-done.5
  455.8 2.6 collective-permute-start.6
  458.4 2.6 collective-permute-done.6
  461.1 5.0 collective-permute-start.7
  466.1 3.5 collective-permute-done.7
  470.3 38.1 %psum.15 = f32[1024]{0:T(1024)S(1)} all-reduce(f32[1024]{0:T(1024)S(1)} %get-tuple-element.2), channel_id=1, replica_groups=mesh['tok'=16,'ch'=16] {'tok'}, use_global_device_ids=true, to_apply=%region_5.6 | all-reduce | flops 1024 | bytes 8192 | tf_op jit(solution)/shard_map/psum | solution.py:105
  (50 shorter events, 21.4 us)
Async XLA Ops:
  7.2 80.8 %copy-start = (bf16[1024,1664]{1,0:T(8,128)(2,1)S(1)}, bf16[1024,1664]{1,0:T(8,128)(2,1)}, u32[]{:S(2)}) copy-start(bf16[1024,1664]{1,0:T(8,128)(2,1)} %param.9) | copy-start | bytes 10223620
  7.2 146.5 %reduce-scatter.4.cloned.1.call-start = ((), (), s32[]{:S(2)}) async-start(), calls=%async_computation.3 | async-start | bytes 7241728 | tf_op jit(solution)/shard_map/reduce_scatter | solution.py:68
  14.6 1.0 copy-start.1
  17.0 1.4 collective-permute-start
  19.2 4.5 collective-permute-start.1
  24.5 5.7 %collective-permute-start.2 = (f32[16,1024]{1,0:T(8,128)S(1)}, f32[16,1024]{1,0:T(8,128)S(1)}, u32[]{:S(2)}, u32[]{:S(2)}) collective-permute-start(f32[16,1024]{1,0:T(8,128)S(1)} %add_select_fusion.5), channel_id=1, source_target_pairs={{0,4},{1,5},{2,6},{3,7},{4,0},{5,1},{6,2},{7,3},{8,12},{9,13},{10,... | collective-permute-start | bytes 196616 | tf_op jit(solution)/shard_map/ppermute | solution.py:14
  30.2 30.4 %collective-permute-start.3 = (f32[16,1024]{1,0:T(8,128)S(1)}, f32[16,1024]{1,0:T(8,128)S(1)}, u32[]{:S(2)}, u32[]{:S(2)}) collective-permute-start(f32[16,1024]{1,0:T(8,128)S(1)} %add_select_fusion.4), channel_id=1, source_target_pairs={{0,8},{1,9},{2,10},{3,11},{4,12},{5,13},{6,14},{7,15},{8,0},{9,1},... | collective-permute-start | bytes 196616 | tf_op jit(solution)/shard_map/ppermute | solution.py:14
  93.4 228.7 %reduce-scatter.6.cloned.1.call-start = ((), (), s32[]{:S(2)}) async-start(), calls=%async_computation.4 | async-start | bytes 1810432 | tf_op jit(solution)/shard_map/reduce_scatter | solution.py:86
  272.2 92.4 %all-gather.2.cloned.1.call-start = ((), (), s32[]{:S(2)}) async-start(), calls=%async_computation.5 | async-start | bytes 1810432 | tf_op jit(solution)/shard_map/all_gather | solution.py:97
  323.8 122.8 %reduce-scatter.8.cloned.1.call-start = ((), (), s32[]{:S(2)}) async-start(), calls=%async_computation.6 | async-start | bytes 1114112 | tf_op jit(solution)/shard_map/reduce_scatter | solution.py:99
  364.6 2.5 copy-start.4
  364.6 2.7 copy-start.5
  367.3 98.8 %copy-start.3 = (s32[1024]{0:T(1024)S(1)}, s32[1024]{0:T(1024)}, u32[]{:S(2)}) copy-start(s32[1024]{0:T(1024)} %param.8) | copy-start | bytes 12292
  367.3 102.3 %copy-start.2 = (s32[16,1024]{1,0:T(8,128)S(1)}, s32[16,1024]{1,0:T(8,128)}, u32[]{:S(2)}) copy-start(s32[16,1024]{1,0:T(8,128)} %param.7) | copy-start | bytes 196612
  450.2 1.3 collective-permute-start.4
  451.4 4.4 collective-permute-start.5
  455.8 5.3 %collective-permute-start.6 = (f32[16,1024]{1,0:T(8,128)S(1)}, f32[16,1024]{1,0:T(8,128)S(1)}, u32[]{:S(2)}, u32[]{:S(2)}) collective-permute-start(f32[16,1024]{1,0:T(8,128)S(1)} %add_select_fusion.2), channel_id=1, source_target_pairs={{0,4},{1,5},{2,6},{3,7},{4,0},{5,1},{6,2},{7,3},{8,12},{9,13},{10,... | collective-permute-start | bytes 196616 | tf_op jit(solution)/shard_map/ppermute | solution.py:14
  461.1 8.5 %collective-permute-start.7 = (f32[16,1024]{1,0:T(8,128)S(1)}, f32[16,1024]{1,0:T(8,128)S(1)}, u32[]{:S(2)}, u32[]{:S(2)}) collective-permute-start(f32[16,1024]{1,0:T(8,128)S(1)} %add_select_fusion.1), channel_id=1, source_target_pairs={{0,8},{1,9},{2,10},{3,11},{4,12},{5,13},{6,14},{7,15},{8,0},{9,1},... | collective-permute-start | bytes 196616 | tf_op jit(solution)/shard_map/ppermute | solution.py:14
Sparse Core Ops, SparseCore 0:
  93.5 60.1 reduce-scatter.3
  272.3 49.7 reduce-scatter.5
  324.1 40.4 all-gather.1
  369.6 76.9 reduce-scatter.7
where the time goes:
time: 516 us
  waiting for transfers between devices  245 us (47%)
  blocking collectives  195 us (38%)
  matrix products  24.3 us (5%)
  starting transfers between devices  19.8 us (4%)
  other arithmetic  16.4 us (3%)
  between operations  13.9 us (3%)
    psum x1, blocking collectives, on_device(): out_tangent = lax.psum(out_part, 'tok').astype(jnp.bfloat16)  88.3 us
    reduce_scatter x1, waiting for transfers between devices, on_device(): lax.psum_scatter(in_part, 'tok', scatter_dimension=0, tiled=True)  77.1 us
    reduce_scatter x1, waiting for transfers between devices, on_device(): lax.psum_scatter(jnp.stack([gate_part, up_part], axis=2), 'ch', scatter_d...  60.3 us
    reduce_scatter x1, waiting for transfers between devices, on_device(): lax.psum_scatter(lax.dot_general(piece, down_weight, (((1,), (1,)), ((),...  49.8 us
    all_gather x1, waiting for transfers between devices, on_device(): piece = lax.all_gather(stacked, 'ch', axis=0, tiled=True)  40.5 us
    psum x1, blocking collectives, on_device(): diagonal_estimate = lax.psum(token_terms, 'tok') / total_rows  38.1 us
    all_gather x1, blocking collectives, on_device(): lax.all_gather(tokens, 'tok', axis=0, tiled=True)  24.4 us
    all_gather x1, blocking collectives, on_device(): lax.all_gather(tangent, 'tok', axis=0, tiled=True)  23.3 us
  transfers between devices with their start and end apart: 12, of which 11 were waited for; matrix products, arithmetic and copies ran while one was open for 0% of the time, Pallas kernels for 0%

commit v1 on v0

v1 whole, which is shorter than its diff:
```python
import math

import jax
import jax.numpy as jnp
import numpy as np
from jax import lax
from jax.sharding import PartitionSpec as P

D = 16384
LANES = 128
F32 = jnp.float32
BF16 = jnp.bfloat16


def sign_table(length):
    table = np.ones((1, 1), np.float32)
    while table.shape[0] < length:
        table = np.block([[table, table], [table, -table]])
    return table


def swap(value, mask):
    pairs = [(source, source ^ mask) for source in range(lax.axis_size("ch"))]
    return lax.ppermute(value, "ch", pairs)


def cross(values, my_index):
    for bit_pos in range(lax.axis_size("ch").bit_length() - 1):
        partner = swap(values, 2**bit_pos)
        upper = (my_index >> bit_pos & 1) == 1
        values = jnp.where(upper, partner - values, values + partner)
    return values


def local_transform(values, table, precision=None):
    rows, length = values.shape
    groups = [values[:, at : at + LANES] for at in range(0, length, LANES)]
    step = 1
    while step < len(groups):
        for low in range(len(groups)):
            if not low & step:
                first, second = groups[low], groups[low + step]
                groups[low], groups[low + step] = first + second, first - second
        step *= 2
    stacked = jnp.concatenate(groups, axis=0)
    done = jnp.dot(stacked, table.astype(values.dtype), precision=precision, preferred_element_type=F32)
    return jnp.concatenate([done[at : at + rows] for at in range(0, done.shape[0], rows)], axis=1)


def gather_tok(value):
    size = lax.axis_size("tok")
    copies = jnp.broadcast_to(value[None], (size,) + value.shape)
    return lax.all_to_all(copies, "tok", 0, 0, tiled=True)


def scatter_tok(value, send_type):
    size = lax.axis_size("tok")
    blocks = value.astype(send_type).reshape(size, value.shape[0] // size, value.shape[1])
    arrived = lax.all_to_all(blocks, "tok", 0, 0, tiled=True)
    return jnp.sum(arrived.astype(F32), axis=0)


def chip_groups():
    size = lax.axis_size("ch")
    return [[chip + core for chip in range(0, size, 2)] for core in range(2)]


def rows_of_core(value, core):
    size = lax.axis_size("ch")
    blocks = value.reshape(size // 2, 2, value.shape[0] // size, value.shape[1])
    chosen = lax.dynamic_index_in_dim(blocks, core, 1, keepdims=False)
    return chosen.reshape(value.shape[0] // 2, value.shape[1])


def scatter_ch(product, rows, core, swap_type, send_type):
    theirs = product(rows_of_core(rows, 1 - core)).astype(swap_type)
    arrived = swap(theirs, 1)
    mine = product(rows_of_core(rows, core))
    both = (mine + arrived.astype(F32)).astype(send_type)
    chips = lax.axis_size("ch") // 2
    blocks = both.reshape(chips, both.shape[0] // chips, both.shape[1])
    pieces = lax.all_to_all(blocks, "ch", 0, 0, tiled=True, axis_index_groups=chip_groups())
    return jnp.sum(pieces.astype(F32), axis=0)


def times(rows, weight):
    return jnp.dot(rows, weight, preferred_element_type=F32)


def times_t(rows, weight):
    return lax.dot_general(rows, weight, (((1,), (1,)), ((), ())), preferred_element_type=F32)


def on_device(tokens, probe, signs, gate_weight, up_weight, down_weight):
    tok_rows, channels = tokens.shape
    total_rows = tok_rows * lax.axis_size("tok")
    hidden = gate_weight.shape[1]
    my_index = lax.axis_index("ch")
    core = my_index & 1
    root_scale = 1.0 / math.sqrt(D)
    table = jnp.asarray(sign_table(LANES))
    probe_signs = (2 * probe - 1).astype(F32)
    channel_signs = (2 * signs - 1).astype(F32)

    all_tokens = gather_tok(tokens).reshape(total_rows, channels)
    token_part = jnp.stack([times(all_tokens, gate_weight), times(all_tokens, up_weight)], axis=1)
    token_sum = lax.psum_scatter(token_part, "ch", scatter_dimension=0, tiled=True)

    crossed = cross((probe_signs * channel_signs[None, :]).astype(BF16), my_index)
    tangent = (local_transform(crossed.astype(F32), table, lax.Precision.HIGHEST) * root_scale).astype(BF16)
    all_tangent = gather_tok(tangent).reshape(total_rows, channels)

    def gate_and_up(rows):
        return jnp.concatenate([times(rows, gate_weight), times(rows, up_weight)], axis=1)

    tangent_sum = scatter_ch(gate_and_up, all_tangent, core, BF16, BF16)

    gate_pre, up_pre = token_sum[:, 0], token_sum[:, 1]
    gate_tan, up_tan = tangent_sum[:, :hidden], tangent_sum[:, hidden:]
    sigmoid_gate = jax.nn.sigmoid(gate_pre)
    activated = gate_pre * sigmoid_gate
    slope_term = sigmoid_gate * (1.0 + gate_pre * (1.0 - sigmoid_gate))
    hidden_tan = (slope_term * gate_tan * up_pre + activated * up_tan).astype(BF16)

    out_part = times(lax.all_gather(hidden_tan, "ch", axis=0, tiled=True), down_weight)
    out_tangent = scatter_tok(out_part, F32).astype(BF16)
    all_out = gather_tok(out_tangent).reshape(total_rows, channels)

    back_hidden = scatter_ch(lambda rows: times_t(rows, down_weight), all_out, core, F32, BF16)
    back_gate = (back_hidden * up_pre * slope_term).astype(BF16)
    back_up = (back_hidden * activated).astype(BF16)
    back = jnp.concatenate([back_gate, back_up], axis=1)
    mine = lax.all_gather(back, "ch", axis=0, tiled=True, axis_index_groups=chip_groups())
    theirs = swap(mine, 1)

    def grad(rows):
        return times_t(rows[:, :hidden], gate_weight) + times_t(rows[:, hidden:], up_weight)

    in_mine, in_theirs = grad(mine), grad(theirs)
    split = (lax.axis_size("ch") // 2, tok_rows, channels)
    in_mine, in_theirs = in_mine.reshape(split), in_theirs.reshape(split)
    first = core == 0
    in_part = jnp.stack(
        [jnp.where(first, in_mine, in_theirs), jnp.where(first, in_theirs, in_mine)], axis=1
    ).reshape(total_rows, channels)
    back_tokens = scatter_tok(in_part, F32)

    local_back = local_transform(back_tokens, table, lax.Precision.HIGHEST)
    rotated_product = cross(local_back, my_index) * root_scale * channel_signs[None, :]
    token_terms = jnp.sum(probe_signs * rotated_product, axis=0)
    pieces = gather_tok(token_terms.reshape(-1, LANES))
    pieces = pieces.reshape(lax.axis_size("tok"), channels // LANES, LANES)
    diagonal_estimate = jnp.sum(pieces, axis=0).reshape(channels) / total_rows
    return (rotated_product, diagonal_estimate)


def solution(mesh):
    placed = (
        P("tok", "ch"),
        P("tok", "ch"),
        P("ch"),
        P("ch", "tok"),
        P("ch", "tok"),
        P("tok", "ch"),
    )
    return jax.shard_map(
        on_device, mesh=mesh, in_specs=placed, out_specs=(P("tok", "ch"), P("ch")), check_vma=False
    )
```

time: 516 us -> 311 us (0.60)
  waiting for transfers between devices: 245 us -> 49.6 us
  blocking collectives: 195 us -> 172 us
  starting transfers between devices: 19.8 us -> 28.6 us
  other arithmetic: 16.4 us -> 11.1 us
    reduce_scatter x3 -> x1, waiting for transfers between devices: 187 us -> 7.96 us  [on_device(): lax.psum_scatter(token_part, 'ch', scatter_dimension=0, tiled=True)]
    psum x2 -> x0, blocking collectives: 126 us -> none  [the longest x1 88.3 us: on_device(): out_tangent = lax.psum(out_part, 'tok').astype(jnp.bfloat16)]
    all_to_all x0 -> x6, blocking collectives: none -> 122 us  [the longest x2 51.6 us: scatter_ch(): lax.all_to_all(blocks, 'ch', 0, 0, tiled=True, axis_index_groups=chip_gro...]
    all_gather x1 -> x0, waiting for transfers between devices: 40.5 us -> none  [on_device(): piece = lax.all_gather(stacked, 'ch', axis=0, tiled=True)]
    all_gather x2 -> x1, blocking collectives: 47.7 us -> 27.3 us  [on_device(): lax.all_gather(back, 'ch', axis=0, tiled=True, axis_index_groups=chip_gro...]
    all_to_all x0 -> x2, waiting for transfers between devices: none -> 19.1 us  [gather_tok(): return lax.all_to_all(copies, 'tok', 0, 0, tiled=True)]
    all_to_all x0 -> x2, starting transfers between devices: none -> 11.3 us  [gather_tok(): return lax.all_to_all(copies, 'tok', 0, 0, tiled=True)]
    eq x1 -> x0, other arithmetic: 6.46 us -> none  [sign_table(): return jnp.where(parity % 2 == 0, 1.0, -1.0).astype(jnp.float32)]
  transfers between devices with their start and end apart: 12 -> 14, of which waited for: 11 -> 11; matrix products, arithmetic and copies ran while one was open for 0% -> 5% of each run, Pallas kernels for 0% -> 0%
where the time goes in v1:
time: 311 us; the launch traced here: 309 us
  blocking collectives  172 us (55%)
  waiting for transfers between devices  49.6 us (16%)
  matrix products  28.7 us (9%)
  starting transfers between devices  28.6 us (9%)
  between operations  14.7 us (5%)
  other arithmetic  11.1 us (4%)
  local copies, waits for them, and re-layouts  4.87 us (2%)
    all_to_all x2, blocking collectives, scatter_ch(): lax.all_to_all(blocks, 'ch', 0, 0, tiled=True, axis_index_groups=chip_gro...  51.6 us
    all_to_all x2, blocking collectives, scatter_tok(): arrived = lax.all_to_all(blocks, 'tok', 0, 0, tiled=True)  45.5 us
    all_gather x1, blocking collectives, on_device(): lax.all_gather(back, 'ch', axis=0, tiled=True, axis_index_groups=chip_gro...  27.3 us
    all_to_all x2, blocking collectives, gather_tok(): return lax.all_to_all(copies, 'tok', 0, 0, tiled=True)  25 us
    ppermute x11, waiting for transfers between devices, swap(): return lax.ppermute(value, 'ch', pairs)  22.6 us
    all_gather x1, blocking collectives, on_device(): lax.all_gather(hidden_tan, 'ch', axis=0, tiled=True)  22.3 us
    all_to_all x2, waiting for transfers between devices, gather_tok(): return lax.all_to_all(copies, 'tok', 0, 0, tiled=True)  19.1 us
    ppermute x11, starting transfers between devices, swap(): return lax.ppermute(value, 'ch', pairs)  17.2 us
  transfers between devices with their start and end apart: 14, of which 11 were waited for; matrix products, arithmetic and copies ran while one was open for 5% of the time, Pallas kernels for 0%

profile of v1, /device:TPU:32, one launch (start us, length us, event | category | flops | bytes accessed | tf_op | source)
XLA Modules:
  0.0 309.0 jit_solution(1250894216051346519)
XLA Ops:
  15.2 3.4 %collective-permute-start.2 = (bf16[16,1024]{1,0:T(8,128)(2,1)S(1)}, bf16[16,1024]{1,0:T(8,128)(2,1)S(1)}, u32[]{:S(2)}, u32[]{:S(2)}) collective-permute-start(bf16[16,1024]{1,0:T(8,128)(2,1)S(1)} %add_select_fusion.4), channel_id=1, source_target_pairs={{0,4},{1,5},{2,6},{3,7},{4,0},{5,1},{6,2},{7,3},{8,12},{9,13},{10,... | collective-permute-start | bytes 98312 | tf_op jit(solution)/shard_map/ppermute | solution.py:24
  20.5 6.0 %collective-permute-start.3 = (bf16[16,1024]{1,0:T(8,128)(2,1)S(1)}, bf16[16,1024]{1,0:T(8,128)(2,1)S(1)}, u32[]{:S(2)}, u32[]{:S(2)}) collective-permute-start(bf16[16,1024]{1,0:T(8,128)(2,1)S(1)} %add_select_fusion.3), channel_id=1, source_target_pairs={{0,8},{1,9},{2,10},{3,11},{4,12},{5,13},{6,14},{7,15},{8,0},{9,1},... | collective-permute-start | bytes 98312 | tf_op jit(solution)/shard_map/ppermute | solution.py:24
  28.1 7.1 %all-to-all-start = ((bf16[16,16,1024]{2,1,0:T(8,128)(2,1)}), bf16[16,16,1024]{2,1,0:T(8,128)(2,1)}, u32[]{:S(2)}, u32[]{:S(2)}) async-start(bf16[16,16,1024]{2,1,0:T(8,128)(2,1)} %broadcast_in_dim.10), calls=%async_computation | async-start | bytes 1048576 | tf_op jit(solution)/shard_map/all_to_all | solution.py:53
  36.5 8.9 %all-to-all-done = bf16[16,16,1024]{2,1,0:T(8,128)(2,1)} async-done(((bf16[16,16,1024]{2,1,0:T(8,128)(2,1)}), bf16[16,16,1024]{2,1,0:T(8,128)(2,1)}, u32[]{:S(2)}, u32[]{:S(2)}) %all-to-all-start) | async-done | bytes 524320 | tf_op jit(solution)/shard_map/all_to_all | solution.py:53
  45.4 3.2 %convolution_bitcast_fusion = f32[256,1,1664]{2,0,1:T(8,128)S(1)} fusion(bf16[256,1024]{1,0:T(8,128)(2,1)} %bitcast, bf16[1024,1664]{1,0:T(8,128)(2,1)} %param.11), kind=kOutput, calls=%fused_computation.1 | convolution fusion | flops 872415232 | bytes 5636096 | tf_op jit(solution)/shard_map/dot_general | solution.py:87
  53.7 4.2 %all-to-all-start.1 = ((bf16[16,16,1024]{2,1,0:T(8,128)(2,1)}), bf16[16,16,1024]{2,1,0:T(8,128)(2,1)}, u32[]{:S(2)}, u32[]{:S(2)}) async-start(bf16[16,16,1024]{2,1,0:T(8,128)(2,1)} %broadcast_in_dim.11), calls=%async_computation.2 | async-start | bytes 1048576 | tf_op jit(solution)/shard_map/all_to_all | solution.py:53
  58.0 10.1 %all-to-all-done.1 = bf16[16,16,1024]{2,1,0:T(8,128)(2,1)} async-done(((bf16[16,16,1024]{2,1,0:T(8,128)(2,1)}), bf16[16,16,1024]{2,1,0:T(8,128)(2,1)}, u32[]{:S(2)}, u32[]{:S(2)}) %all-to-all-start.1) | async-done | bytes 524320 | tf_op jit(solution)/shard_map/all_to_all | solution.py:53
  69.2 2.7 convolution_convert_fusion
  75.4 30.9 %all_to_all.40 = bf16[8,16,3328]{2,1,0:T(8,128)(2,1)S(1)} all-to-all(bf16[8,16,3328]{2,1,0:T(8,128)(2,1)S(1)} %bitcast.71), channel_id=1, replica_groups={{0,2,4,6,8,10,12,14},{1,3,5,7,9,11,13,15},{16,18,20,22,24,26,28,30},{17..., dimensions={0} | all-to-all | bytes 1703936 | tf_op jit(solution)/shard_map/all_to_all | solution.py:82
  107.1 8.0 %reduce-scatter.2.cloned.1.call-done = f32[16,2,1664]{2,0,1:T(8,128)} async-done(((f32[256,2,1664]{2,0,1:T(8,128)}), f32[16,2,1664]{2,0,1:T(8,128)}) %reduce-scatter.2.cloned.1.call-update) | async-done | bytes 213008 | tf_op jit(solution)/shard_map/reduce_scatter | solution.py:107
  116.2 22.3 %all_gather.6 = bf16[256,1664]{1,0:T(8,128)(2,1)S(1)} all-gather(bf16[16,1664]{1,0:T(8,128)(2,1)S(1)} %fusion.9), channel_id=1, replica_groups=mesh['tok'=16,'ch'=16] {'ch'}, dimensions={0}, use_global_device_ids=true | all-gather | bytes 905216 | tf_op jit(solution)/shard_map/all_gather | solution.py:125
  138.5 3.1 %fusion.15 = f32[256,1024]{1,0:T(8,128)S(1)} fusion(bf16[256,1664]{1,0:T(8,128)(2,1)S(1)} %all_gather.6, bf16[1664,1024]{1,0:T(8,128)(2,1)} %param.12), kind=kOutput, calls=%fused_computation.106 | convolution fusion | flops 872415232 | bytes 5308416 | tf_op jit(solution)/shard_map/dot_general | solution.py:87
  141.6 24.0 %all_to_all.41 = f32[16,16,1024]{2,1,0:T(8,128)} all-to-all(f32[16,16,1024]{2,1,0:T(8,128)S(1)} %bitcast.82), channel_id=1, replica_groups=mesh['tok'=16,'ch'=16] {'tok'}, dimensions={0} | all-to-all | bytes 2097152 | tf_op jit(solution)/shard_map/all_to_all | solution.py:59
  166.9 14.2 %all_to_all.42 = bf16[16,16,1024]{2,1,0:T(8,128)(2,1)S(1)} all-to-all(bf16[16,16,1024]{2,1,0:T(8,128)(2,1)S(1)} %broadcast_in_dim.12), channel_id=1, replica_groups=mesh['tok'=16,'ch'=16] {'tok'}, dimensions={0} | all-to-all | bytes 1048576 | tf_op jit(solution)/shard_map/all_to_all | solution.py:53
  181.2 3.2 %fusion.16 = f32[128,1664]{1,0:T(8,128)S(1)} fusion(bf16[128,1024]{1,0:T(8,128)(2,1)S(1)} %bitcast.81, bf16[1664,1024]{1,0:T(8,128)(2,1)} %param.12), kind=kOutput, calls=%fused_computation.107 | convolution fusion | flops 436207616 | bytes 4521984 | tf_op jit(solution)/shard_map/dot_general | solution.py:91
  188.3 20.7 %all_to_all.43 = bf16[8,16,1664]{2,1,0:T(8,128)(2,1)S(1)} all-to-all(bf16[8,16,1664]{2,1,0:T(8,128)(2,1)S(1)} %bitcast.79), channel_id=1, replica_groups={{0,2,4,6,8,10,12,14},{1,3,5,7,9,11,13,15},{16,18,20,22,24,26,28,30},{17..., dimensions={0} | all-to-all | bytes 851968 | tf_op jit(solution)/shard_map/all_to_all | solution.py:82
  209.1 27.3 %all_gather.7 = bf16[128,3328]{1,0:T(8,128)(2,1)} all-gather(bf16[16,3328]{1,0:T(8,128)(2,1)S(1)} %pad_maximum_fusion.3), channel_id=1, replica_groups={{0,2,4,6,8,10,12,14},{1,3,5,7,9,11,13,15},{16,18,20,22,24,26,28,30},{17..., dimensions={0}, use_global_device_ids=true | all-gather | bytes 958464 | tf_op jit(solution)/shard_map/all_gather | solution.py:133
  236.4 2.4 fusion.6
  245.6 21.5 %all_to_all.44 = f32[16,16,1024]{2,1,0:T(8,128)} all-to-all(f32[16,16,1024]{2,1,0:T(8,128)S(1)} %bitcast.70), channel_id=1, replica_groups=mesh['tok'=16,'ch'=16] {'tok'}, dimensions={0} | all-to-all | bytes 2097152 | tf_op jit(solution)/shard_map/all_to_all | solution.py:59
  271.0 2.5 collective-permute-start.8
  273.5 2.4 collective-permute-done.8
  276.8 4.4 %collective-permute-done.9 = f32[16,1024]{1,0:T(8,128)S(1)} collective-permute-done((f32[16,1024]{1,0:T(8,128)S(1)}, f32[16,1024]{1,0:T(8,128)S(1)}, u32[]{:S(2)}, u32[]{:S(2)}) %collective-permute-start.9) | collective-permute-done | bytes 65568 | tf_op jit(solution)/shard_map/ppermute | solution.py:24
  283.2 7.0 %collective-permute-done.10 = f32[16,1024]{1,0:T(8,128)S(1)} collective-permute-done((f32[16,1024]{1,0:T(8,128)S(1)}, f32[16,1024]{1,0:T(8,128)S(1)}, u32[]{:S(2)}, u32[]{:S(2)}) %collective-permute-start.10) | collective-permute-done | bytes 65568 | tf_op jit(solution)/shard_map/ppermute | solution.py:24
  290.8 10.7 %all_to_all.45 = f32[16,8,128]{2,1,0:T(8,128)S(1)} all-to-all(f32[16,8,128]{2,1,0:T(8,128)S(1)} %broadcast_in_dim.14), channel_id=1, replica_groups=mesh['tok'=16,'ch'=16] {'tok'}, dimensions={0} | all-to-all | bytes 131072 | tf_op jit(solution)/shard_map/all_to_all | solution.py:53
  (105 shorter events, 44.3 us)
Async XLA Ops:
  7.2 41.5 %copy-start = (bf16[1024,1664]{1,0:T(8,128)(2,1)S(1)}, bf16[1024,1664]{1,0:T(8,128)(2,1)}, u32[]{:S(2)}) copy-start(bf16[1024,1664]{1,0:T(8,128)(2,1)} %param.10) | copy-start | bytes 10223620
  9.1 1.3 collective-permute-start
  11.2 4.0 %collective-permute-start.1 = (bf16[16,1024]{1,0:T(8,128)(2,1)S(1)}, bf16[16,1024]{1,0:T(8,128)(2,1)S(1)}, u32[]{:S(2)}, u32[]{:S(2)}) collective-permute-start(bf16[16,1024]{1,0:T(8,128)(2,1)S(1)} %add_select_fusion.5), channel_id=1, source_target_pairs={{0,2},{1,3},{2,0},{3,1},{4,6},{5,7},{6,4},{7,5},{8,10},{9,11},{10,... | collective-permute-start | bytes 98312 | tf_op jit(solution)/shard_map/ppermute | solution.py:24
  15.2 5.3 %collective-permute-start.2 = (bf16[16,1024]{1,0:T(8,128)(2,1)S(1)}, bf16[16,1024]{1,0:T(8,128)(2,1)S(1)}, u32[]{:S(2)}, u32[]{:S(2)}) collective-permute-start(bf16[16,1024]{1,0:T(8,128)(2,1)S(1)} %add_select_fusion.4), channel_id=1, source_target_pairs={{0,4},{1,5},{2,6},{3,7},{4,0},{5,1},{6,2},{7,3},{8,12},{9,13},{10,... | collective-permute-start | bytes 98312 | tf_op jit(solution)/shard_map/ppermute | solution.py:24
  20.5 14.8 %collective-permute-start.3 = (bf16[16,1024]{1,0:T(8,128)(2,1)S(1)}, bf16[16,1024]{1,0:T(8,128)(2,1)S(1)}, u32[]{:S(2)}, u32[]{:S(2)}) collective-permute-start(bf16[16,1024]{1,0:T(8,128)(2,1)S(1)} %add_select_fusion.3), channel_id=1, source_target_pairs={{0,8},{1,9},{2,10},{3,11},{4,12},{5,13},{6,14},{7,15},{8,0},{9,1},... | collective-permute-start | bytes 98312 | tf_op jit(solution)/shard_map/ppermute | solution.py:24
  28.1 17.3 %all-to-all-start = ((bf16[16,16,1024]{2,1,0:T(8,128)(2,1)}), bf16[16,16,1024]{2,1,0:T(8,128)(2,1)}, u32[]{:S(2)}, u32[]{:S(2)}) async-start(bf16[16,16,1024]{2,1,0:T(8,128)(2,1)} %broadcast_in_dim.10), calls=%async_computation | async-start | bytes 1048576 | tf_op jit(solution)/shard_map/all_to_all | solution.py:53
  35.2 79.8 %reduce-scatter.2.cloned.1.call-start = ((), (), s32[]{:S(2)}) async-start(), calls=%async_computation.9 | async-start | bytes 3620864 | tf_op jit(solution)/shard_map/reduce_scatter | solution.py:107
  53.7 14.4 %all-to-all-start.1 = ((bf16[16,16,1024]{2,1,0:T(8,128)(2,1)}), bf16[16,16,1024]{2,1,0:T(8,128)(2,1)}, u32[]{:S(2)}, u32[]{:S(2)}) async-start(bf16[16,16,1024]{2,1,0:T(8,128)(2,1)} %broadcast_in_dim.11), calls=%async_computation.2 | async-start | bytes 1048576 | tf_op jit(solution)/shard_map/all_to_all | solution.py:53
  72.5 2.0 copy-start.1
  72.6 2.6 collective-permute-start.4
  166.9 20.1 %copy-start.3 = (bf16[1664,1024]{1,0:T(8,128)(2,1)S(1)}, bf16[1664,1024]{1,0:T(8,128)(2,1)}, u32[]{:S(2)}) copy-start(bf16[1664,1024]{1,0:T(8,128)(2,1)} %param.12) | copy-start | bytes 10223620
  184.4 24.6 %copy-start.4 = (f32[16,2,1664]{2,0,1:T(8,128)S(1)}, f32[16,2,1664]{2,0,1:T(8,128)}, u32[]{:S(2)}) copy-start(f32[16,2,1664]{2,0,1:T(8,128)} %reduce-scatter.2.cloned.1.call-done) | copy-start | bytes 638980
  184.4 2.6 collective-permute-start.5
  236.4 4.6 %collective-permute-start.6 = (bf16[128,3328]{1,0:T(8,128)(2,1)}, bf16[128,3328]{1,0:T(8,128)(2,1)}, u32[]{:S(2)}, u32[]{:S(2)}) collective-permute-start(bf16[128,3328]{1,0:T(8,128)(2,1)} %all_gather.7), channel_id=1, source_target_pairs={{0,1},{1,0},{2,3},{3,2},{4,5},{5,4},{6,7},{7,6},{8,9},{9,8},{10,11... | collective-permute-start | bytes 2555912 | tf_op jit(solution)/shard_map/ppermute | solution.py:24
  236.4 2.4 copy-start.2
  245.5 37.6 %copy-start.6 = (s32[1024]{0:T(1024)S(1)}, s32[1024]{0:T(1024)}, u32[]{:S(2)}) copy-start(s32[1024]{0:T(1024)} %param.9) | copy-start | bytes 12292
  245.5 44.6 %copy-start.5 = (s32[16,1024]{1,0:T(8,128)S(1)}, s32[16,1024]{1,0:T(8,128)}, u32[]{:S(2)}) copy-start(s32[16,1024]{1,0:T(8,128)} %param.8) | copy-start | bytes 196612
  269.6 1.3 collective-permute-start.7
  271.0 4.9 %collective-permute-start.8 = (f32[16,1024]{1,0:T(8,128)S(1)}, f32[16,1024]{1,0:T(8,128)S(1)}, u32[]{:S(2)}, u32[]{:S(2)}) collective-permute-start(f32[16,1024]{1,0:T(8,128)S(1)} %add_select_fusion.2), channel_id=1, source_target_pairs={{0,2},{1,3},{2,0},{3,1},{4,6},{5,7},{6,4},{7,5},{8,10},{9,11},{10,... | collective-permute-start | bytes 196616 | tf_op jit(solution)/shard_map/ppermute | solution.py:24
  275.9 5.3 %collective-permute-start.9 = (f32[16,1024]{1,0:T(8,128)S(1)}, f32[16,1024]{1,0:T(8,128)S(1)}, u32[]{:S(2)}, u32[]{:S(2)}) collective-permute-start(f32[16,1024]{1,0:T(8,128)S(1)} %add_select_fusion.1), channel_id=1, source_target_pairs={{0,4},{1,5},{2,6},{3,7},{4,0},{5,1},{6,2},{7,3},{8,12},{9,13},{10,... | collective-permute-start | bytes 196616 | tf_op jit(solution)/shard_map/ppermute | solution.py:24
  281.2 9.0 %collective-permute-start.10 = (f32[16,1024]{1,0:T(8,128)S(1)}, f32[16,1024]{1,0:T(8,128)S(1)}, u32[]{:S(2)}, u32[]{:S(2)}) collective-permute-start(f32[16,1024]{1,0:T(8,128)S(1)} %add_select_fusion), channel_id=1, source_target_pairs={{0,8},{1,9},{2,10},{3,11},{4,12},{5,13},{6,14},{7,15},{8,0},{9,1},... | collective-permute-start | bytes 196616 | tf_op jit(solution)/shard_map/ppermute | solution.py:24
Sparse Core Ops, SparseCore 0:
  52.9 62.0 reduce-scatter.1

commit v2 on v1

--- a/solution.py
+++ b/solution.py
@@ -24,8 +24,8 @@
     return lax.ppermute(value, "ch", pairs)
 
 
-def cross(values, my_index):
-    for bit_pos in range(lax.axis_size("ch").bit_length() - 1):
+def cross(values, my_index, bits):
+    for bit_pos in bits:
         partner = swap(values, 2**bit_pos)
         upper = (my_index >> bit_pos & 1) == 1
         values = jnp.where(upper, partner - values, values + partner)
@@ -83,6 +83,15 @@
     return jnp.sum(pieces.astype(F32), axis=0)
 
 
+def gather_ch(value, core):
+    chips = lax.axis_size("ch") // 2
+    copies = jnp.broadcast_to(value[None], (chips,) + value.shape)
+    mine = lax.all_to_all(copies, "ch", 0, 0, tiled=True, axis_index_groups=chip_groups())
+    theirs = swap(mine, 1)
+    first = core == 0
+    return jnp.stack([jnp.where(first, mine, theirs), jnp.where(first, theirs, mine)], axis=1)
+
+
 def times(rows, weight):
     return jnp.dot(rows, weight, preferred_element_type=F32)
 
@@ -102,11 +111,14 @@
     probe_signs = (2 * probe - 1).astype(F32)
     channel_signs = (2 * signs - 1).astype(F32)
 
+    bits = list(range(lax.axis_size("ch").bit_length() - 1))
     all_tokens = gather_tok(tokens).reshape(total_rows, channels)
+    crossed = cross((probe_signs * channel_signs[None, :]).astype(BF16), my_index, bits[:-1])
+    crossed, all_tokens = lax.optimization_barrier((crossed, all_tokens))
     token_part = jnp.stack([times(all_tokens, gate_weight), times(all_tokens, up_weight)], axis=1)
+    crossed = cross(crossed, my_index, bits[-1:])
+    crossed, _ = lax.optimization_barrier((crossed, token_part))
     token_sum = lax.psum_scatter(token_part, "ch", scatter_dimension=0, tiled=True)
-
-    crossed = cross((probe_signs * channel_signs[None, :]).astype(BF16), my_index)
     tangent = (local_transform(crossed.astype(F32), table, lax.Precision.HIGHEST) * root_scale).astype(BF16)
     all_tangent = gather_tok(tangent).reshape(total_rows, channels)
 
@@ -123,30 +135,19 @@
     hidden_tan = (slope_term * gate_tan * up_pre + activated * up_tan).astype(BF16)
 
     out_part = times(lax.all_gather(hidden_tan, "ch", axis=0, tiled=True), down_weight)
-    out_tangent = scatter_tok(out_part, F32).astype(BF16)
+    out_tangent = scatter_tok(out_part, BF16).astype(BF16)
     all_out = gather_tok(out_tangent).reshape(total_rows, channels)
 
     back_hidden = scatter_ch(lambda rows: times_t(rows, down_weight), all_out, core, F32, BF16)
     back_gate = (back_hidden * up_pre * slope_term).astype(BF16)
     back_up = (back_hidden * activated).astype(BF16)
     back = jnp.concatenate([back_gate, back_up], axis=1)
-    mine = lax.all_gather(back, "ch", axis=0, tiled=True, axis_index_groups=chip_groups())
-    theirs = swap(mine, 1)
-
-    def grad(rows):
-        return times_t(rows[:, :hidden], gate_weight) + times_t(rows[:, hidden:], up_weight)
-
-    in_mine, in_theirs = grad(mine), grad(theirs)
-    split = (lax.axis_size("ch") // 2, tok_rows, channels)
-    in_mine, in_theirs = in_mine.reshape(split), in_theirs.reshape(split)
-    first = core == 0
-    in_part = jnp.stack(
-        [jnp.where(first, in_mine, in_theirs), jnp.where(first, in_theirs, in_mine)], axis=1
-    ).reshape(total_rows, channels)
-    back_tokens = scatter_tok(in_part, F32)
+    all_back = gather_ch(back, core).reshape(total_rows, 2 * hidden)
+    in_part = times_t(all_back[:, :hidden], gate_weight) + times_t(all_back[:, hidden:], up_weight)
+    back_tokens = scatter_tok(in_part, BF16)
 
     local_back = local_transform(back_tokens, table, lax.Precision.HIGHEST)
-    rotated_product = cross(local_back, my_index) * root_scale * channel_signs[None, :]
+    rotated_product = cross(local_back, my_index, bits) * root_scale * channel_signs[None, :]
     token_terms = jnp.sum(probe_signs * rotated_product, axis=0)
     pieces = gather_tok(token_terms.reshape(-1, LANES))
     pieces = pieces.reshape(lax.axis_size("tok"), channels // LANES, LANES)

time: 311 us -> 287 us (0.923)
  blocking collectives: 172 us -> 159 us
  matrix products: 28.7 us -> 20.2 us
    all_gather x1 -> x0, blocking collectives: 27.3 us -> none  [on_device(): lax.all_gather(back, 'ch', axis=0, tiled=True, axis_index_groups=chip_gro...]
    all_to_all x0 -> x1, blocking collectives: none -> 26.8 us  [gather_ch(): lax.all_to_all(copies, 'ch', 0, 0, tiled=True, axis_index_groups=chip_gro...]
    all_to_all x2, blocking collectives: 45.5 us -> 33.9 us  [scatter_tok(): arrived = lax.all_to_all(blocks, 'tok', 0, 0, tiled=True)]
    dot_general x6 -> x4, matrix products: 13.5 us -> 6.71 us  [times_t(): lax.dot_general(rows, weight, (((1,), (1,)), ((), ())), preferred_element...]
  transfers between devices with their start and end apart: 14 -> 14, of which waited for: 11 -> 11; matrix products, arithmetic and copies ran while one was open for 5% -> 6% of each run, Pallas kernels for 0% -> 0%
where the time goes in v2:
time: 287 us; the launch traced here: 285 us
  blocking collectives  159 us (55%)
  waiting for transfers between devices  47.1 us (16%)
  starting transfers between devices  25.9 us (9%)
  matrix products  20.2 us (7%)
  between operations  14.6 us (5%)
  other arithmetic  11.3 us (4%)
  local copies, waits for them, and re-layouts  6.42 us (2%)
    all_to_all x2, blocking collectives, scatter_ch(): lax.all_to_all(blocks, 'ch', 0, 0, tiled=True, axis_index_groups=chip_gro...  52.2 us
    all_to_all x2, blocking collectives, scatter_tok(): arrived = lax.all_to_all(blocks, 'tok', 0, 0, tiled=True)  33.9 us
    all_to_all x1, blocking collectives, gather_ch(): lax.all_to_all(copies, 'ch', 0, 0, tiled=True, axis_index_groups=chip_gro...  26.8 us
    all_to_all x2, blocking collectives, gather_tok(): return lax.all_to_all(copies, 'tok', 0, 0, tiled=True)  24.8 us
    ppermute x11, waiting for transfers between devices, swap(): return lax.ppermute(value, 'ch', pairs)  24.3 us
    all_gather x1, blocking collectives, on_device(): lax.all_gather(hidden_tan, 'ch', axis=0, tiled=True)  21.5 us
    all_to_all x2, waiting for transfers between devices, gather_tok(): return lax.all_to_all(copies, 'tok', 0, 0, tiled=True)  16.7 us
    ppermute x11, starting transfers between devices, swap(): return lax.ppermute(value, 'ch', pairs)  16.3 us
  transfers between devices with their start and end apart: 14, of which 11 were waited for; matrix products, arithmetic and copies ran while one was open for 6% of the time, Pallas kernels for 0%

profile of v2, /device:TPU:32, one launch (start us, length us, event | category | flops | bytes accessed | tf_op | source)
XLA Modules:
  0.0 284.9 jit_solution(14764976036292788120)
XLA Ops:
  14.8 5.3 %all-to-all-start = ((bf16[16,16,1024]{2,1,0:T(8,128)(2,1)}), bf16[16,16,1024]{2,1,0:T(8,128)(2,1)}, u32[]{:S(2)}, u32[]{:S(2)}) async-start(bf16[16,16,1024]{2,1,0:T(8,128)(2,1)} %broadcast_in_dim.12), calls=%async_computation | async-start | bytes 1048576 | tf_op jit(solution)/shard_map/all_to_all | solution.py:53
  20.2 3.4 %collective-permute-start.2 = (bf16[16,1024]{1,0:T(8,128)(2,1)S(1)}, bf16[16,1024]{1,0:T(8,128)(2,1)S(1)}, u32[]{:S(2)}, u32[]{:S(2)}) collective-permute-start(bf16[16,1024]{1,0:T(8,128)(2,1)S(1)} %add_select_fusion.5), channel_id=1, source_target_pairs={{0,4},{1,5},{2,6},{3,7},{4,0},{5,1},{6,2},{7,3},{8,12},{9,13},{10,... | collective-permute-start | bytes 98312 | tf_op jit(solution)/shard_map/ppermute | solution.py:24
  25.5 6.5 %all-to-all-done = bf16[16,16,1024]{2,1,0:T(8,128)(2,1)} async-done(((bf16[16,16,1024]{2,1,0:T(8,128)(2,1)}), bf16[16,16,1024]{2,1,0:T(8,128)(2,1)}, u32[]{:S(2)}, u32[]{:S(2)}) %all-to-all-start) | async-done | bytes 524320 | tf_op jit(solution)/shard_map/all_to_all | solution.py:53
  32.0 7.0 %collective-permute-start.3 = (bf16[16,1024]{1,0:T(8,128)(2,1)S(1)}, bf16[16,1024]{1,0:T(8,128)(2,1)S(1)}, u32[]{:S(2)}, u32[]{:S(2)}) collective-permute-start(bf16[16,1024]{1,0:T(8,128)(2,1)S(1)} %add_select_fusion.4), channel_id=1, source_target_pairs={{0,8},{1,9},{2,10},{3,11},{4,12},{5,13},{6,14},{7,15},{8,0},{9,1},... | collective-permute-start | bytes 98312 | tf_op jit(solution)/shard_map/ppermute | solution.py:24
  39.0 3.2 %convolution_bitcast_fusion = f32[256,1,1664]{2,0,1:T(8,128)S(1)} fusion(bf16[256,1024]{1,0:T(8,128)(2,1)} %bitcast, bf16[1024,1664]{1,0:T(8,128)(2,1)} %param.11), kind=kOutput, calls=%fused_computation.1 | convolution fusion | flops 872415232 | bytes 5636096 | tf_op jit(solution)/shard_map/dot_general | solution.py:96
  48.3 4.2 %all-to-all-start.1 = ((bf16[16,16,1024]{2,1,0:T(8,128)(2,1)}), bf16[16,16,1024]{2,1,0:T(8,128)(2,1)}, u32[]{:S(2)}, u32[]{:S(2)}) async-start(bf16[16,16,1024]{2,1,0:T(8,128)(2,1)} %broadcast_in_dim.13), calls=%async_computation.2 | async-start | bytes 1048576 | tf_op jit(solution)/shard_map/all_to_all | solution.py:53
  52.6 10.2 %all-to-all-done.1 = bf16[16,16,1024]{2,1,0:T(8,128)(2,1)} async-done(((bf16[16,16,1024]{2,1,0:T(8,128)(2,1)}), bf16[16,16,1024]{2,1,0:T(8,128)(2,1)}, u32[]{:S(2)}, u32[]{:S(2)}) %all-to-all-start.1) | async-done | bytes 524320 | tf_op jit(solution)/shard_map/all_to_all | solution.py:53
  63.9 2.6 convolution_convert_fusion
  70.0 31.7 %all_to_all.45 = bf16[8,16,3328]{2,1,0:T(8,128)(2,1)S(1)} all-to-all(bf16[8,16,3328]{2,1,0:T(8,128)(2,1)S(1)} %bitcast.69), channel_id=1, replica_groups={{0,2,4,6,8,10,12,14},{1,3,5,7,9,11,13,15},{16,18,20,22,24,26,28,30},{17..., dimensions={0} | all-to-all | bytes 1703936 | tf_op jit(solution)/shard_map/all_to_all | solution.py:82
  102.5 6.1 %reduce-scatter.2.cloned.1.call-done = f32[16,2,1664]{2,0,1:T(8,128)} async-done(((f32[256,2,1664]{2,0,1:T(8,128)}), f32[16,2,1664]{2,0,1:T(8,128)}) %reduce-scatter.2.cloned.1.call-update) | async-done | bytes 213008 | tf_op jit(solution)/shard_map/reduce_scatter | solution.py:121
  109.7 21.5 %all_gather.3 = bf16[256,1664]{1,0:T(8,128)(2,1)S(1)} all-gather(bf16[16,1664]{1,0:T(8,128)(2,1)S(1)} %fusion.7), channel_id=1, replica_groups=mesh['tok'=16,'ch'=16] {'ch'}, dimensions={0}, use_global_device_ids=true | all-gather | bytes 905216 | tf_op jit(solution)/shard_map/all_gather | solution.py:137
  131.2 3.1 %convolution_convert_fusion.2 = bf16[256,1024]{1,0:T(8,128)(2,1)S(1)} fusion(bf16[256,1664]{1,0:T(8,128)(2,1)S(1)} %all_gather.3, bf16[1664,1024]{1,0:T(8,128)(2,1)} %param.12), kind=kOutput, calls=%fused_computation.12 | convolution fusion | flops 872677376 | bytes 4784128 | tf_op jit(solution)/shard_map/dot_general | solution.py:96
  134.4 19.1 %all_to_all.46 = bf16[16,16,1024]{2,1,0:T(8,128)(2,1)} all-to-all(bf16[16,16,1024]{2,1,0:T(8,128)(2,1)S(1)} %bitcast.81), channel_id=1, replica_groups=mesh['tok'=16,'ch'=16] {'tok'}, dimensions={0} | all-to-all | bytes 1048576 | tf_op jit(solution)/shard_map/all_to_all | solution.py:59
  154.7 14.2 %all_to_all.47 = bf16[16,16,1024]{2,1,0:T(8,128)(2,1)S(1)} all-to-all(bf16[16,16,1024]{2,1,0:T(8,128)(2,1)S(1)} %broadcast_in_dim.14), channel_id=1, replica_groups=mesh['tok'=16,'ch'=16] {'tok'}, dimensions={0} | all-to-all | bytes 1048576 | tf_op jit(solution)/shard_map/all_to_all | solution.py:53
  168.9 3.2 %fusion.13 = f32[128,1664]{1,0:T(8,128)S(1)} fusion(bf16[128,1024]{1,0:T(8,128)(2,1)S(1)} %bitcast.79, bf16[1664,1024]{1,0:T(8,128)(2,1)} %param.12), kind=kOutput, calls=%fused_computation.105 | convolution fusion | flops 436207616 | bytes 4521984 | tf_op jit(solution)/shard_map/dot_general | solution.py:100
  172.4 2.4 collective-permute-done.5
  176.0 20.5 %all_to_all.48 = bf16[8,16,1664]{2,1,0:T(8,128)(2,1)S(1)} all-to-all(bf16[8,16,1664]{2,1,0:T(8,128)(2,1)S(1)} %bitcast.75), channel_id=1, replica_groups={{0,2,4,6,8,10,12,14},{1,3,5,7,9,11,13,15},{16,18,20,22,24,26,28,30},{17..., dimensions={0} | all-to-all | bytes 851968 | tf_op jit(solution)/shard_map/all_to_all | solution.py:82
  196.8 26.8 %all_to_all.49 = bf16[8,16,3328]{2,1,0:T(8,128)(2,1)} all-to-all(bf16[8,16,3328]{2,1,0:T(8,128)(2,1)S(1)} %broadcast_in_dim.15), channel_id=1, replica_groups={{0,2,4,6,8,10,12,14},{1,3,5,7,9,11,13,15},{16,18,20,22,24,26,28,30},{17..., dimensions={0} | all-to-all | bytes 1703936 | tf_op jit(solution)/shard_map/all_to_all | solution.py:89
  223.6 2.7 collective-permute-done.6
  231.1 14.8 %all_to_all.50 = bf16[16,16,1024]{2,1,0:T(8,128)(2,1)S(1)} all-to-all(bf16[16,16,1024]{2,1,0:T(8,128)(2,1)S(1)} %bitcast.80), channel_id=1, replica_groups=mesh['tok'=16,'ch'=16] {'tok'}, dimensions={0} | all-to-all | bytes 1048576 | tf_op jit(solution)/shard_map/all_to_all | solution.py:59
  249.3 2.8 collective-permute-done.8
  252.6 4.9 %collective-permute-done.9 = f32[16,1024]{1,0:T(8,128)S(1)} collective-permute-done((f32[16,1024]{1,0:T(8,128)S(1)}, f32[16,1024]{1,0:T(8,128)S(1)}, u32[]{:S(2)}, u32[]{:S(2)}) %collective-permute-start.9) | collective-permute-done | bytes 65568 | tf_op jit(solution)/shard_map/ppermute | solution.py:24
  259.0 7.2 %collective-permute-done.10 = f32[16,1024]{1,0:T(8,128)S(1)} collective-permute-done((f32[16,1024]{1,0:T(8,128)S(1)}, f32[16,1024]{1,0:T(8,128)S(1)}, u32[]{:S(2)}, u32[]{:S(2)}) %collective-permute-start.10) | collective-permute-done | bytes 65568 | tf_op jit(solution)/shard_map/ppermute | solution.py:24
  266.9 10.6 %all_to_all.51 = f32[16,8,128]{2,1,0:T(8,128)S(1)} all-to-all(f32[16,8,128]{2,1,0:T(8,128)S(1)} %broadcast_in_dim.17), channel_id=1, replica_groups=mesh['tok'=16,'ch'=16] {'tok'}, dimensions={0} | all-to-all | bytes 131072 | tf_op jit(solution)/shard_map/all_to_all | solution.py:53
  (108 shorter events, 36.1 us)
Async XLA Ops:
  7.2 35.1 %copy-start = (bf16[1024,1664]{1,0:T(8,128)(2,1)S(1)}, bf16[1024,1664]{1,0:T(8,128)(2,1)}, u32[]{:S(2)}) copy-start(bf16[1024,1664]{1,0:T(8,128)(2,1)} %param.10) | copy-start | bytes 10223620
  9.1 1.3 collective-permute-start
  11.2 9.0 %collective-permute-start.1 = (bf16[16,1024]{1,0:T(8,128)(2,1)S(1)}, bf16[16,1024]{1,0:T(8,128)(2,1)S(1)}, u32[]{:S(2)}, u32[]{:S(2)}) collective-permute-start(bf16[16,1024]{1,0:T(8,128)(2,1)S(1)} %add_select_fusion.6), channel_id=1, source_target_pairs={{0,2},{1,3},{2,0},{3,1},{4,6},{5,7},{6,4},{7,5},{8,10},{9,11},{10,... | collective-permute-start | bytes 98312 | tf_op jit(solution)/shard_map/ppermute | solution.py:24
  14.8 17.2 %all-to-all-start = ((bf16[16,16,1024]{2,1,0:T(8,128)(2,1)}), bf16[16,16,1024]{2,1,0:T(8,128)(2,1)}, u32[]{:S(2)}, u32[]{:S(2)}) async-start(bf16[16,16,1024]{2,1,0:T(8,128)(2,1)} %broadcast_in_dim.12), calls=%async_computation | async-start | bytes 1048576 | tf_op jit(solution)/shard_map/all_to_all | solution.py:53
  20.1 88.5 %reduce-scatter.2.cloned.1.call-start = ((), (), s32[]{:S(2)}) async-start(), calls=%async_computation.10 | async-start | bytes 3620864 | tf_op jit(solution)/shard_map/reduce_scatter | solution.py:121
  20.2 5.3 %collective-permute-start.2 = (bf16[16,1024]{1,0:T(8,128)(2,1)S(1)}, bf16[16,1024]{1,0:T(8,128)(2,1)S(1)}, u32[]{:S(2)}, u32[]{:S(2)}) collective-permute-start(bf16[16,1024]{1,0:T(8,128)(2,1)S(1)} %add_select_fusion.5), channel_id=1, source_target_pairs={{0,4},{1,5},{2,6},{3,7},{4,0},{5,1},{6,2},{7,3},{8,12},{9,13},{10,... | collective-permute-start | bytes 98312 | tf_op jit(solution)/shard_map/ppermute | solution.py:24
  32.0 14.4 %collective-permute-start.3 = (bf16[16,1024]{1,0:T(8,128)(2,1)S(1)}, bf16[16,1024]{1,0:T(8,128)(2,1)S(1)}, u32[]{:S(2)}, u32[]{:S(2)}) collective-permute-start(bf16[16,1024]{1,0:T(8,128)(2,1)S(1)} %add_select_fusion.4), channel_id=1, source_target_pairs={{0,8},{1,9},{2,10},{3,11},{4,12},{5,13},{6,14},{7,15},{8,0},{9,1},... | collective-permute-start | bytes 98312 | tf_op jit(solution)/shard_map/ppermute | solution.py:24
  46.3 0.8 copy-start.6
  48.3 14.5 %all-to-all-start.1 = ((bf16[16,16,1024]{2,1,0:T(8,128)(2,1)}), bf16[16,16,1024]{2,1,0:T(8,128)(2,1)}, u32[]{:S(2)}, u32[]{:S(2)}) async-start(bf16[16,16,1024]{2,1,0:T(8,128)(2,1)} %broadcast_in_dim.13), calls=%async_computation.2 | async-start | bytes 1048576 | tf_op jit(solution)/shard_map/all_to_all | solution.py:53
  67.2 2.0 copy-start.2
  67.3 2.6 collective-permute-start.4
  154.7 20.1 %copy-start.1 = (bf16[1664,1024]{1,0:T(8,128)(2,1)S(1)}, bf16[1664,1024]{1,0:T(8,128)(2,1)}, u32[]{:S(2)}) copy-start(bf16[1664,1024]{1,0:T(8,128)(2,1)} %param.12) | copy-start | bytes 10223620
  172.1 24.5 %copy-start.4 = (f32[16,2,1664]{2,0,1:T(8,128)S(1)}, f32[16,2,1664]{2,0,1:T(8,128)}, u32[]{:S(2)}) copy-start(f32[16,2,1664]{2,0,1:T(8,128)} %reduce-scatter.2.cloned.1.call-done) | copy-start | bytes 638980
  172.1 2.6 collective-permute-start.5
  223.6 2.7 collective-permute-start.6
  228.0 2.0 copy-start.3
  230.0 29.0 %copy-start.7 = (s32[1024]{0:T(1024)S(1)}, s32[1024]{0:T(1024)}, u32[]{:S(2)}) copy-start(s32[1024]{0:T(1024)} %param.9) | copy-start | bytes 12292
  230.0 36.2 %copy-start.5 = (s32[16,1024]{1,0:T(8,128)S(1)}, s32[16,1024]{1,0:T(8,128)}, u32[]{:S(2)}) copy-start(s32[16,1024]{1,0:T(8,128)} %param.8) | copy-start | bytes 196612
  246.4 1.3 collective-permute-start.7
  247.8 4.4 %collective-permute-start.8 = (f32[16,1024]{1,0:T(8,128)S(1)}, f32[16,1024]{1,0:T(8,128)S(1)}, u32[]{:S(2)}, u32[]{:S(2)}) collective-permute-start(f32[16,1024]{1,0:T(8,128)S(1)} %add_select_fusion.2), channel_id=1, source_target_pairs={{0,2},{1,3},{2,0},{3,1},{4,6},{5,7},{6,4},{7,5},{8,10},{9,11},{10,... | collective-permute-start | bytes 196616 | tf_op jit(solution)/shard_map/ppermute | solution.py:24
  252.1 5.4 %collective-permute-start.9 = (f32[16,1024]{1,0:T(8,128)S(1)}, f32[16,1024]{1,0:T(8,128)S(1)}, u32[]{:S(2)}, u32[]{:S(2)}) collective-permute-start(f32[16,1024]{1,0:T(8,128)S(1)} %add_select_fusion.1), channel_id=1, source_target_pairs={{0,4},{1,5},{2,6},{3,7},{4,0},{5,1},{6,2},{7,3},{8,12},{9,13},{10,... | collective-permute-start | bytes 196616 | tf_op jit(solution)/shard_map/ppermute | solution.py:24
  257.5 8.7 %collective-permute-start.10 = (f32[16,1024]{1,0:T(8,128)S(1)}, f32[16,1024]{1,0:T(8,128)S(1)}, u32[]{:S(2)}, u32[]{:S(2)}) collective-permute-start(f32[16,1024]{1,0:T(8,128)S(1)} %add_select_fusion), channel_id=1, source_target_pairs={{0,8},{1,9},{2,10},{3,11},{4,12},{5,13},{6,14},{7,15},{8,0},{9,1},... | collective-permute-start | bytes 196616 | tf_op jit(solution)/shard_map/ppermute | solution.py:24
Sparse Core Ops, SparseCore 0:
  46.5 62.0 reduce-scatter.1

commit v3 on v2

--- a/solution.py
+++ b/solution.py
@@ -10,6 +10,7 @@
 LANES = 128
 F32 = jnp.float32
 BF16 = jnp.bfloat16
+F16 = jnp.float16
 
 
 def sign_table(length):
@@ -24,12 +25,23 @@
     return lax.ppermute(value, "ch", pairs)
 
 
+def bit_sign(my_index, bit_pos, dtype):
+    return (1 - 2 * (my_index >> bit_pos & 1)).astype(dtype)
+
+
 def cross(values, my_index, bits):
     for bit_pos in bits:
-        partner = swap(values, 2**bit_pos)
-        upper = (my_index >> bit_pos & 1) == 1
-        values = jnp.where(upper, partner - values, values + partner)
+        values = swap(values, 2**bit_pos) + values * bit_sign(my_index, bit_pos, values.dtype)
     return values
+
+
+def cross_two(values, my_index, low, high):
+    low_sign = bit_sign(my_index, low, values.dtype)
+    high_sign = bit_sign(my_index, high, values.dtype)
+    both = swap(values, 2**low + 2**high)
+    from_high = swap(values, 2**high)
+    from_low = swap(values, 2**low)
+    return (both + from_high * low_sign) + (from_low * high_sign + values * (low_sign * high_sign))
 
 
 def local_transform(values, table, precision=None):
@@ -72,24 +84,39 @@
     return chosen.reshape(value.shape[0] // 2, value.shape[1])
 
 
-def scatter_ch(product, rows, core, swap_type, send_type):
-    theirs = product(rows_of_core(rows, 1 - core)).astype(swap_type)
-    arrived = swap(theirs, 1)
-    mine = product(rows_of_core(rows, core))
-    both = (mine + arrived.astype(F32)).astype(send_type)
-    chips = lax.axis_size("ch") // 2
-    blocks = both.reshape(chips, both.shape[0] // chips, both.shape[1])
-    pieces = lax.all_to_all(blocks, "ch", 0, 0, tiled=True, axis_index_groups=chip_groups())
-    return jnp.sum(pieces.astype(F32), axis=0)
+def sum_on_chip(products, rows, core):
+    their_rows, my_rows = rows_of_core(rows, 1 - core), rows_of_core(rows, core)
+    arrived = [swap(product(their_rows), 1) for product in products]
+    return [product(my_rows) + other for product, other in zip(products, arrived)]
 
 
-def gather_ch(value, core):
+def to_chips(value):
     chips = lax.axis_size("ch") // 2
-    copies = jnp.broadcast_to(value[None], (chips,) + value.shape)
-    mine = lax.all_to_all(copies, "ch", 0, 0, tiled=True, axis_index_groups=chip_groups())
-    theirs = swap(mine, 1)
-    first = core == 0
-    return jnp.stack([jnp.where(first, mine, theirs), jnp.where(first, theirs, mine)], axis=1)
+    blocks = value.reshape(chips, value.shape[0] // chips, value.shape[1])
+    return lax.all_to_all(blocks, "ch", 0, 0, tiled=True, axis_index_groups=chip_groups())
+
+
+def pack(parts):
+    lane = lax.broadcasted_iota(jnp.int32, (parts[0].shape[0], LANES), 1)
+    scaled, exponents = [], jnp.zeros(lane.shape, F32)
+    for at, part in enumerate(parts):
+        peak = jnp.max(jnp.abs(part), axis=1, keepdims=True)
+        exponent = jnp.clip(jnp.round(jnp.log2(peak)), -120.0, 120.0)
+        scaled.append((part * jnp.exp2(-exponent)).astype(F16))
+        exponents = jnp.where(lane == at, exponent, exponents)
+    return jnp.concatenate(scaled + [exponents.astype(F16)], axis=1)
+
+
+def unpack_sum(pieces, count):
+    width = (pieces.shape[2] - LANES) // count
+    tail = lax.optimization_barrier(pieces[:, :, count * width :]).astype(F32)
+    lane = lax.broadcasted_iota(jnp.int32, tail.shape, 2)
+    sums = []
+    for at in range(count):
+        exponent = jnp.sum(jnp.where(lane == at, tail, 0.0), axis=2, keepdims=True)
+        part = pieces[:, :, at * width : (at + 1) * width].astype(F32)
+        sums.append(jnp.sum(part * jnp.exp2(exponent), axis=0))
+    return sums
 
 
 def times(rows, weight):
@@ -111,43 +138,43 @@
     probe_signs = (2 * probe - 1).astype(F32)
     channel_signs = (2 * signs - 1).astype(F32)
 
-    bits = list(range(lax.axis_size("ch").bit_length() - 1))
     all_tokens = gather_tok(tokens).reshape(total_rows, channels)
-    crossed = cross((probe_signs * channel_signs[None, :]).astype(BF16), my_index, bits[:-1])
+    crossed = cross((probe_signs * channel_signs[None, :]).astype(BF16), my_index, (0, 1, 2))
     crossed, all_tokens = lax.optimization_barrier((crossed, all_tokens))
     token_part = jnp.stack([times(all_tokens, gate_weight), times(all_tokens, up_weight)], axis=1)
-    crossed = cross(crossed, my_index, bits[-1:])
+    crossed = cross(crossed, my_index, (3,))
     crossed, _ = lax.optimization_barrier((crossed, token_part))
     token_sum = lax.psum_scatter(token_part, "ch", scatter_dimension=0, tiled=True)
     tangent = (local_transform(crossed.astype(F32), table, lax.Precision.HIGHEST) * root_scale).astype(BF16)
     all_tangent = gather_tok(tangent).reshape(total_rows, channels)
-
-    def gate_and_up(rows):
-        return jnp.concatenate([times(rows, gate_weight), times(rows, up_weight)], axis=1)
-
-    tangent_sum = scatter_ch(gate_and_up, all_tangent, core, BF16, BF16)
+    gate_and_up = [lambda rows: times(rows, gate_weight), lambda rows: times(rows, up_weight)]
+    tangent_pieces = to_chips(pack(sum_on_chip(gate_and_up, all_tangent, core)))
 
     gate_pre, up_pre = token_sum[:, 0], token_sum[:, 1]
-    gate_tan, up_tan = tangent_sum[:, :hidden], tangent_sum[:, hidden:]
+    gate_tan, up_tan = unpack_sum(tangent_pieces, 2)
     sigmoid_gate = jax.nn.sigmoid(gate_pre)
     activated = gate_pre * sigmoid_gate
     slope_term = sigmoid_gate * (1.0 + gate_pre * (1.0 - sigmoid_gate))
     hidden_tan = (slope_term * gate_tan * up_pre + activated * up_tan).astype(BF16)
 
+    factors = jnp.concatenate([(up_pre * slope_term).astype(BF16), activated.astype(BF16)], axis=1)
+    all_factors = lax.all_gather(factors, "ch", axis=0, tiled=True)
+
     out_part = times(lax.all_gather(hidden_tan, "ch", axis=0, tiled=True), down_weight)
     out_tangent = scatter_tok(out_part, BF16).astype(BF16)
     all_out = gather_tok(out_tangent).reshape(total_rows, channels)
 
-    back_hidden = scatter_ch(lambda rows: times_t(rows, down_weight), all_out, core, F32, BF16)
-    back_gate = (back_hidden * up_pre * slope_term).astype(BF16)
-    back_up = (back_hidden * activated).astype(BF16)
-    back = jnp.concatenate([back_gate, back_up], axis=1)
-    all_back = gather_ch(back, core).reshape(total_rows, 2 * hidden)
-    in_part = times_t(all_back[:, :hidden], gate_weight) + times_t(all_back[:, hidden:], up_weight)
+    back_part = sum_on_chip([lambda rows: times_t(rows, down_weight)], all_out, core)[0]
+    back_hidden = jnp.sum(to_chips(back_part.astype(BF16)).astype(F32), axis=0)
+    all_back = lax.all_gather(back_hidden.astype(BF16), "ch", axis=0, tiled=True).astype(F32)
+    back_gate = (all_back * all_factors[:, :hidden].astype(F32)).astype(BF16)
+    back_up = (all_back * all_factors[:, hidden:].astype(F32)).astype(BF16)
+    in_part = times_t(back_gate, gate_weight) + times_t(back_up, up_weight)
     back_tokens = scatter_tok(in_part, BF16)
 
     local_back = local_transform(back_tokens, table, lax.Precision.HIGHEST)
-    rotated_product = cross(local_back, my_index, bits) * root_scale * channel_signs[None, :]
+    local_back = cross_two(cross(local_back, my_index, (0, 1)), my_index, 2, 3)
+    rotated_product = local_back * root_scale * channel_signs[None, :]
     token_terms = jnp.sum(probe_signs * rotated_product, axis=0)
     pieces = gather_tok(token_terms.reshape(-1, LANES))
     pieces = pieces.reshape(lax.axis_size("tok"), channels // LANES, LANES)

time: 287 us -> 283 us (0.986)
  blocking collectives: 159 us -> 142 us
  starting transfers between devices: 25.9 us -> 34.6 us
  other arithmetic: 11.3 us -> 15.1 us
    all_to_all x3 -> x2, blocking collectives: 79 us -> 56.7 us  [to_chips(): lax.all_to_all(blocks, 'ch', 0, 0, tiled=True, axis_index_groups=chip_gro...]
    all_gather x0 -> x1, blocking collectives: none -> 18.5 us  [on_device(): lax.all_gather(back_hidden.astype(BF16), 'ch', axis=0, tiled=True)]
    all_to_all x2 -> x1, blocking collectives: 24.8 us -> 10.5 us  [gather_tok(): return lax.all_to_all(copies, 'tok', 0, 0, tiled=True)]
    all_to_all x2 -> x3, waiting for transfers between devices: 16.7 us -> 26.7 us  [gather_tok(): return lax.all_to_all(copies, 'tok', 0, 0, tiled=True)]
    ppermute x11 -> x12, waiting for transfers between devices: 24.3 us -> 15.8 us  [swap(): return lax.ppermute(value, 'ch', pairs)]
    all_to_all x2 -> x3, starting transfers between devices: 9.59 us -> 13.9 us  [gather_tok(): return lax.all_to_all(copies, 'tok', 0, 0, tiled=True)]
    ppermute x11 -> x12, starting transfers between devices: 16.3 us -> 20.4 us  [swap(): return lax.ppermute(value, 'ch', pairs)]
  transfers between devices with their start and end apart: 14 -> 17, of which waited for: 11 -> 13; matrix products, arithmetic and copies ran while one was open for 6% -> 8% of each run, Pallas kernels for 0% -> 0%
where the time goes in v3:
time: 283 us; the launch traced here: 282 us
  blocking collectives  142 us (50%)
  waiting for transfers between devices  47.5 us (17%)
  starting transfers between devices  34.6 us (12%)
  matrix products  20.1 us (7%)
  other arithmetic  15.1 us (5%)
  between operations  14.7 us (5%)
  local copies, waits for them, and re-layouts  7.73 us (3%)
    all_to_all x2, blocking collectives, to_chips(): lax.all_to_all(blocks, 'ch', 0, 0, tiled=True, axis_index_groups=chip_gro...  56.7 us
    all_to_all x2, blocking collectives, scatter_tok(): arrived = lax.all_to_all(blocks, 'tok', 0, 0, tiled=True)  35.1 us
    all_to_all x3, waiting for transfers between devices, gather_tok(): return lax.all_to_all(copies, 'tok', 0, 0, tiled=True)  26.7 us
    all_gather x1, blocking collectives, on_device(): lax.all_gather(hidden_tan, 'ch', axis=0, tiled=True)  21.5 us
    ppermute x12, starting transfers between devices, swap(): return lax.ppermute(value, 'ch', pairs)  20.4 us
    all_gather x1, blocking collectives, on_device(): lax.all_gather(back_hidden.astype(BF16), 'ch', axis=0, tiled=True)  18.5 us
    ppermute x12, waiting for transfers between devices, swap(): return lax.ppermute(value, 'ch', pairs)  15.8 us
    all_to_all x3, starting transfers between devices, gather_tok(): return lax.all_to_all(copies, 'tok', 0, 0, tiled=True)  13.9 us
  transfers between devices with their start and end apart: 17, of which 13 were waited for; matrix products, arithmetic and copies ran while one was open for 8% of the time, Pallas kernels for 0%

profile of v3, /device:TPU:32, one launch (start us, length us, event | category | flops | bytes accessed | tf_op | source)
XLA Modules:
  0.0 282.0 jit_solution(2091891717679442304)
XLA Ops:
  14.8 5.3 %all-to-all-start = ((bf16[16,16,1024]{2,1,0:T(8,128)(2,1)}), bf16[16,16,1024]{2,1,0:T(8,128)(2,1)}, u32[]{:S(2)}, u32[]{:S(2)}) async-start(bf16[16,16,1024]{2,1,0:T(8,128)(2,1)} %broadcast_in_dim.52), calls=%async_computation | async-start | bytes 1048576 | tf_op jit(solution)/shard_map/all_to_all | solution.py:65
  20.2 3.4 %collective-permute-start.2 = (bf16[16,1024]{1,0:T(8,128)(2,1)S(1)}, bf16[16,1024]{1,0:T(8,128)(2,1)S(1)}, u32[]{:S(2)}, u32[]{:S(2)}) collective-permute-start(bf16[16,1024]{1,0:T(8,128)(2,1)S(1)} %multiply_add_fusion.5), channel_id=1, source_target_pairs={{0,4},{1,5},{2,6},{3,7},{4,0},{5,1},{6,2},{7,3},{8,12},{9,13},{10,... | collective-permute-start | bytes 98312 | tf_op jit(solution)/shard_map/ppermute | solution.py:25
  25.5 6.5 %all-to-all-done = bf16[16,16,1024]{2,1,0:T(8,128)(2,1)} async-done(((bf16[16,16,1024]{2,1,0:T(8,128)(2,1)}), bf16[16,16,1024]{2,1,0:T(8,128)(2,1)}, u32[]{:S(2)}, u32[]{:S(2)}) %all-to-all-start) | async-done | bytes 524320 | tf_op jit(solution)/shard_map/all_to_all | solution.py:65
  32.0 7.0 %collective-permute-start.3 = (bf16[16,1024]{1,0:T(8,128)(2,1)S(1)}, bf16[16,1024]{1,0:T(8,128)(2,1)S(1)}, u32[]{:S(2)}, u32[]{:S(2)}) collective-permute-start(bf16[16,1024]{1,0:T(8,128)(2,1)S(1)} %multiply_add_fusion.4), channel_id=1, source_target_pairs={{0,8},{1,9},{2,10},{3,11},{4,12},{5,13},{6,14},{7,15},{8,0},{9,1},... | collective-permute-start | bytes 98312 | tf_op jit(solution)/shard_map/ppermute | solution.py:25
  39.0 3.2 %convolution_bitcast_fusion = f32[256,1,1664]{2,0,1:T(8,128)S(1)} fusion(bf16[256,1024]{1,0:T(8,128)(2,1)} %bitcast, bf16[1024,1664]{1,0:T(8,128)(2,1)} %param.11), kind=kOutput, calls=%fused_computation.1 | convolution fusion | flops 872415232 | bytes 5636096 | tf_op jit(solution)/shard_map/dot_general | solution.py:123
  48.3 4.3 %all-to-all-start.1 = ((bf16[16,16,1024]{2,1,0:T(8,128)(2,1)}), bf16[16,16,1024]{2,1,0:T(8,128)(2,1)}, u32[]{:S(2)}, u32[]{:S(2)}) async-start(bf16[16,16,1024]{2,1,0:T(8,128)(2,1)} %broadcast_in_dim.53), calls=%async_computation.2 | async-start | bytes 1048576 | tf_op jit(solution)/shard_map/all_to_all | solution.py:65
  52.6 10.2 %all-to-all-done.1 = bf16[16,16,1024]{2,1,0:T(8,128)(2,1)} async-done(((bf16[16,16,1024]{2,1,0:T(8,128)(2,1)}), bf16[16,16,1024]{2,1,0:T(8,128)(2,1)}, u32[]{:S(2)}, u32[]{:S(2)}) %all-to-all-start.1) | async-done | bytes 524320 | tf_op jit(solution)/shard_map/all_to_all | solution.py:65
  70.0 32.8 %all_to_all.40 = f16[8,16,3456]{2,1,0:T(8,128)(2,1)S(1)} all-to-all(f16[8,16,3456]{2,1,0:T(8,128)(2,1)S(1)} %bitcast.62), channel_id=1, replica_groups={{0,2,4,6,8,10,12,14},{1,3,5,7,9,11,13,15},{16,18,20,22,24,26,28,30},{17..., dimensions={0} | all-to-all | bytes 1769472 | tf_op jit(solution)/shard_map/all_to_all | solution.py:96
  103.8 5.0 %reduce-scatter.2.cloned.1.call-done = f32[16,2,1664]{2,0,1:T(8,128)} async-done(((f32[256,2,1664]{2,0,1:T(8,128)}), f32[16,2,1664]{2,0,1:T(8,128)}) %reduce-scatter.2.cloned.1.call-update) | async-done | bytes 213008 | tf_op jit(solution)/shard_map/reduce_scatter | solution.py:147
  110.4 21.5 %all_gather.9 = bf16[256,1664]{1,0:T(8,128)(2,1)S(1)} all-gather(bf16[16,1664]{1,0:T(8,128)(2,1)S(1)} %get-tuple-element.43), channel_id=1, replica_groups=mesh['tok'=16,'ch'=16] {'ch'}, dimensions={0}, use_global_device_ids=true | all-gather | bytes 905216 | tf_op jit(solution)/shard_map/all_gather | solution.py:163
  132.0 3.1 %convolution_convert_fusion = bf16[256,1024]{1,0:T(8,128)(2,1)S(1)} fusion(bf16[256,1664]{1,0:T(8,128)(2,1)S(1)} %all_gather.9, bf16[1664,1024]{1,0:T(8,128)(2,1)} %param.12), kind=kOutput, calls=%fused_computation.12 | convolution fusion | flops 872677376 | bytes 4784128 | tf_op jit(solution)/shard_map/dot_general | solution.py:123
  135.1 19.4 %all_to_all.41 = bf16[16,16,1024]{2,1,0:T(8,128)(2,1)} all-to-all(bf16[16,16,1024]{2,1,0:T(8,128)(2,1)S(1)} %bitcast.71), channel_id=1, replica_groups=mesh['tok'=16,'ch'=16] {'tok'}, dimensions={0} | all-to-all | bytes 1048576 | tf_op jit(solution)/shard_map/all_to_all | solution.py:71
  156.5 4.3 %all-to-all-start.4 = ((bf16[16,16,1024]{2,1,0:T(8,128)(2,1)}), bf16[16,16,1024]{2,1,0:T(8,128)(2,1)}, u32[]{:S(2)}, u32[]{:S(2)}) async-start(bf16[16,16,1024]{2,1,0:T(8,128)(2,1)} %broadcast_in_dim.58), calls=%async_computation.5 | async-start | bytes 1048576 | tf_op jit(solution)/shard_map/all_to_all | solution.py:65
  161.7 10.0 %all-to-all-done.4 = bf16[16,16,1024]{2,1,0:T(8,128)(2,1)} async-done(((bf16[16,16,1024]{2,1,0:T(8,128)(2,1)}), bf16[16,16,1024]{2,1,0:T(8,128)(2,1)}, u32[]{:S(2)}, u32[]{:S(2)}) %all-to-all-start.4) | async-done | bytes 524320 | tf_op jit(solution)/shard_map/all_to_all | solution.py:65
  172.9 3.2 %fusion.16 = f32[128,1664]{1,0:T(8,128)S(1)} fusion(bf16[128,1024]{1,0:T(8,128)(2,1)S(1)} %bitcast.69, bf16[1664,1024]{1,0:T(8,128)(2,1)} %param.12), kind=kOutput, calls=%fused_computation.116 | convolution fusion | flops 436207616 | bytes 4521984 | tf_op jit(solution)/shard_map/dot_general | solution.py:127
  176.2 2.4 collective-permute-done.6
  179.8 24.0 %all_to_all.42 = bf16[8,16,1664]{2,1,0:T(8,128)(2,1)} all-to-all(bf16[8,16,1664]{2,1,0:T(8,128)(2,1)S(1)} %bitcast.67), channel_id=1, replica_groups={{0,2,4,6,8,10,12,14},{1,3,5,7,9,11,13,15},{16,18,20,22,24,26,28,30},{17..., dimensions={0} | all-to-all | bytes 851968 | tf_op jit(solution)/shard_map/all_to_all | solution.py:96
  204.9 18.5 %all_gather.10 = bf16[256,1664]{1,0:T(8,128)(2,1)} all-gather(bf16[16,1664]{1,0:T(8,128)(2,1)S(1)} %reduce_sum.92), channel_id=1, replica_groups=mesh['tok'=16,'ch'=16] {'ch'}, dimensions={0}, use_global_device_ids=true | all-gather | bytes 905216 | tf_op jit(solution)/shard_map/all_gather | solution.py:169
  223.3 2.7 fusion.5
  227.8 15.7 %all_to_all.43 = bf16[16,16,1024]{2,1,0:T(8,128)(2,1)S(1)} all-to-all(bf16[16,16,1024]{2,1,0:T(8,128)(2,1)S(1)} %bitcast.70), channel_id=1, replica_groups=mesh['tok'=16,'ch'=16] {'tok'}, dimensions={0} | all-to-all | bytes 1048576 | tf_op jit(solution)/shard_map/all_to_all | solution.py:71
  247.1 3.7 %collective-permute-done.8 = f32[16,1024]{1,0:T(8,128)} collective-permute-done((f32[16,1024]{1,0:T(8,128)S(1)}, f32[16,1024]{1,0:T(8,128)}, u32[]{:S(2)}, u32[]{:S(2)}) %collective-permute-start.8) | collective-permute-done | bytes 65568 | tf_op jit(solution)/shard_map/ppermute | solution.py:25
  255.6 2.7 collective-permute-start.9
  258.2 2.9 %collective-permute-done.10 = f32[16,1024]{1,0:T(8,128)} collective-permute-done((f32[16,1024]{1,0:T(8,128)S(1)}, f32[16,1024]{1,0:T(8,128)}, u32[]{:S(2)}, u32[]{:S(2)}) %collective-permute-start.10) | collective-permute-done | bytes 65568 | tf_op jit(solution)/shard_map/ppermute | solution.py:25
  264.1 10.5 %all_to_all.44 = f32[16,8,128]{2,1,0:T(8,128)S(1)} all-to-all(f32[16,8,128]{2,1,0:T(8,128)S(1)} %broadcast_in_dim.60), channel_id=1, replica_groups=mesh['tok'=16,'ch'=16] {'tok'}, dimensions={0} | all-to-all | bytes 131072 | tf_op jit(solution)/shard_map/all_to_all | solution.py:65
  (129 shorter events, 45.3 us)
Async XLA Ops:
  7.2 35.0 %copy-start = (bf16[1024,1664]{1,0:T(8,128)(2,1)S(1)}, bf16[1024,1664]{1,0:T(8,128)(2,1)}, u32[]{:S(2)}) copy-start(bf16[1024,1664]{1,0:T(8,128)(2,1)} %param.10) | copy-start | bytes 10223620
  9.1 1.3 collective-permute-start
  11.2 9.0 %collective-permute-start.1 = (bf16[16,1024]{1,0:T(8,128)(2,1)S(1)}, bf16[16,1024]{1,0:T(8,128)(2,1)S(1)}, u32[]{:S(2)}, u32[]{:S(2)}) collective-permute-start(bf16[16,1024]{1,0:T(8,128)(2,1)S(1)} %multiply_add_fusion.6), channel_id=1, source_target_pairs={{0,2},{1,3},{2,0},{3,1},{4,6},{5,7},{6,4},{7,5},{8,10},{9,11},{10,... | collective-permute-start | bytes 98312 | tf_op jit(solution)/shard_map/ppermute | solution.py:25
  14.8 17.2 %all-to-all-start = ((bf16[16,16,1024]{2,1,0:T(8,128)(2,1)}), bf16[16,16,1024]{2,1,0:T(8,128)(2,1)}, u32[]{:S(2)}, u32[]{:S(2)}) async-start(bf16[16,16,1024]{2,1,0:T(8,128)(2,1)} %broadcast_in_dim.52), calls=%async_computation | async-start | bytes 1048576 | tf_op jit(solution)/shard_map/all_to_all | solution.py:65
  20.1 88.6 %reduce-scatter.2.cloned.1.call-start = ((), (), s32[]{:S(2)}) async-start(), calls=%async_computation.9 | async-start | bytes 3620864 | tf_op jit(solution)/shard_map/reduce_scatter | solution.py:147
  20.2 5.3 %collective-permute-start.2 = (bf16[16,1024]{1,0:T(8,128)(2,1)S(1)}, bf16[16,1024]{1,0:T(8,128)(2,1)S(1)}, u32[]{:S(2)}, u32[]{:S(2)}) collective-permute-start(bf16[16,1024]{1,0:T(8,128)(2,1)S(1)} %multiply_add_fusion.5), channel_id=1, source_target_pairs={{0,4},{1,5},{2,6},{3,7},{4,0},{5,1},{6,2},{7,3},{8,12},{9,13},{10,... | collective-permute-start | bytes 98312 | tf_op jit(solution)/shard_map/ppermute | solution.py:25
  32.0 14.4 %collective-permute-start.3 = (bf16[16,1024]{1,0:T(8,128)(2,1)S(1)}, bf16[16,1024]{1,0:T(8,128)(2,1)S(1)}, u32[]{:S(2)}, u32[]{:S(2)}) collective-permute-start(bf16[16,1024]{1,0:T(8,128)(2,1)S(1)} %multiply_add_fusion.4), channel_id=1, source_target_pairs={{0,8},{1,9},{2,10},{3,11},{4,12},{5,13},{6,14},{7,15},{8,0},{9,1},... | collective-permute-start | bytes 98312 | tf_op jit(solution)/shard_map/ppermute | solution.py:25
  48.3 14.5 %all-to-all-start.1 = ((bf16[16,16,1024]{2,1,0:T(8,128)(2,1)}), bf16[16,16,1024]{2,1,0:T(8,128)(2,1)}, u32[]{:S(2)}, u32[]{:S(2)}) async-start(bf16[16,16,1024]{2,1,0:T(8,128)(2,1)} %broadcast_in_dim.53), calls=%async_computation.2 | async-start | bytes 1048576 | tf_op jit(solution)/shard_map/all_to_all | solution.py:65
  64.7 2.5 collective-permute-start.4
  65.6 2.9 %collective-permute-start.5 = (f32[128,1664]{1,0:T(8,128)S(1)}, f32[128,1664]{1,0:T(8,128)S(1)}, u32[]{:S(2)}, u32[]{:S(2)}) collective-permute-start(f32[128,1664]{1,0:T(8,128)S(1)} %fusion.15), channel_id=1, source_target_pairs={{0,1},{1,0},{2,3},{3,2},{4,5},{5,4},{6,7},{7,6},{8,9},{9,8},{10,11... | collective-permute-start | bytes 2555912 | tf_op jit(solution)/shard_map/ppermute | solution.py:25
  132.0 29.0 %copy-start.9 = (bf16[16,1664]{1,0:T(8,128)(2,1)S(1)}, bf16[16,1664]{1,0:T(8,128)(2,1)}, u32[]{:S(2)}) copy-start(bf16[16,1664]{1,0:T(8,128)(2,1)} %get-tuple-element.42) | copy-start | bytes 159748
  132.0 29.1 %copy-start.10 = (bf16[16,1664]{1,0:T(8,128)(2,1)S(1)}, bf16[16,1664]{1,0:T(8,128)(2,1)}, u32[]{:S(2)}) copy-start(bf16[16,1664]{1,0:T(8,128)(2,1)} %get-tuple-element.44) | copy-start | bytes 159748
  156.5 15.2 %all-to-all-start.4 = ((bf16[16,16,1024]{2,1,0:T(8,128)(2,1)}), bf16[16,16,1024]{2,1,0:T(8,128)(2,1)}, u32[]{:S(2)}, u32[]{:S(2)}) async-start(bf16[16,16,1024]{2,1,0:T(8,128)(2,1)} %broadcast_in_dim.58), calls=%async_computation.5 | async-start | bytes 1048576 | tf_op jit(solution)/shard_map/all_to_all | solution.py:65
  160.8 62.6 %all-gather.2.cloned.1.call-start = ((), (), s32[]{:S(2)}) async-start(), calls=%async_computation.10 | async-start | bytes 1810432 | tf_op jit(solution)/shard_map/all_gather | solution.py:161
  171.7 6.9 %copy-start.1 = (bf16[1664,1024]{1,0:T(8,128)(2,1)S(1)}, bf16[1664,1024]{1,0:T(8,128)(2,1)}, u32[]{:S(2)}) copy-start(bf16[1664,1024]{1,0:T(8,128)(2,1)} %param.12) | copy-start | bytes 10223620
  176.1 2.5 collective-permute-start.6
  226.6 17.0 %copy-start.7 = (f32[128,128]{1,0:T(8,128)S(1)}, f32[128,128]{1,0:T(8,128)}, u32[]{:S(2)}) copy-start(f32[128,128]{1,0:T(8,128)} %constant.60.clone) | copy-start | bytes 196612
  226.6 31.6 %copy-start.12 = (s32[1024]{0:T(1024)S(1)}, s32[1024]{0:T(1024)}, u32[]{:S(2)}) copy-start(s32[1024]{0:T(1024)} %param.9) | copy-start | bytes 12292
  226.6 35.9 %copy-start.5 = (s32[16,1024]{1,0:T(8,128)S(1)}, s32[16,1024]{1,0:T(8,128)}, u32[]{:S(2)}) copy-start(s32[16,1024]{1,0:T(8,128)} %param.8) | copy-start | bytes 196612
  243.9 1.5 collective-permute-start.7
  246.3 4.5 %collective-permute-start.8 = (f32[16,1024]{1,0:T(8,128)S(1)}, f32[16,1024]{1,0:T(8,128)}, u32[]{:S(2)}, u32[]{:S(2)}) collective-permute-start(f32[16,1024]{1,0:T(8,128)S(1)} %multiply_add_fusion.1), channel_id=1, source_target_pairs={{0,2},{1,3},{2,0},{3,1},{4,6},{5,7},{6,4},{7,5},{8,10},{9,11},{10,... | collective-permute-start | bytes 196616 | tf_op jit(solution)/shard_map/ppermute | solution.py:25
  251.7 9.5 %collective-permute-start.10 = (f32[16,1024]{1,0:T(8,128)S(1)}, f32[16,1024]{1,0:T(8,128)}, u32[]{:S(2)}, u32[]{:S(2)}) collective-permute-start(f32[16,1024]{1,0:T(8,128)S(1)} %multiply_add_fusion), channel_id=1, source_target_pairs={{0,8},{1,9},{2,10},{3,11},{4,12},{5,13},{6,14},{7,15},{8,0},{9,1},... | collective-permute-start | bytes 196616 | tf_op jit(solution)/shard_map/ppermute | solution.py:25
  253.4 7.7 %collective-permute-start.11 = (f32[16,1024]{1,0:T(8,128)S(1)}, f32[16,1024]{1,0:T(8,128)}, u32[]{:S(2)}, u32[]{:S(2)}) collective-permute-start(f32[16,1024]{1,0:T(8,128)S(1)} %multiply_add_fusion), channel_id=1, source_target_pairs={{0,4},{1,5},{2,6},{3,7},{4,0},{5,1},{6,2},{7,3},{8,12},{9,13},{10,... | collective-permute-start | bytes 196616 | tf_op jit(solution)/shard_map/ppermute | solution.py:25
  255.6 6.9 %collective-permute-start.9 = (f32[16,1024]{1,0:T(8,128)S(1)}, f32[16,1024]{1,0:T(8,128)}, u32[]{:S(2)}, u32[]{:S(2)}) collective-permute-start(f32[16,1024]{1,0:T(8,128)S(1)} %multiply_add_fusion), channel_id=1, source_target_pairs={{0,12},{1,13},{2,14},{3,15},{4,8},{5,9},{6,10},{7,11},{8,4},{9,5},... | collective-permute-start | bytes 196616 | tf_op jit(solution)/shard_map/ppermute | solution.py:25
  (7 other events, 13.1 us)
Sparse Core Ops, SparseCore 0:
  46.5 62.2 reduce-scatter.1
  163.6 42.4 all-gather.1

commit v4 on v3

--- a/solution.py
+++ b/solution.py
@@ -139,7 +139,8 @@
     channel_signs = (2 * signs - 1).astype(F32)
 
     all_tokens = gather_tok(tokens).reshape(total_rows, channels)
-    crossed = cross((probe_signs * channel_signs[None, :]).astype(BF16), my_index, (0, 1, 2))
+    crossed = cross_two(jnp.where(probe == signs[None, :], 1.0, -1.0).astype(BF16), my_index, 0, 1)
+    crossed = cross(crossed, my_index, (2,))
     crossed, all_tokens = lax.optimization_barrier((crossed, all_tokens))
     token_part = jnp.stack([times(all_tokens, gate_weight), times(all_tokens, up_weight)], axis=1)
     crossed = cross(crossed, my_index, (3,))
@@ -164,7 +165,8 @@
     out_tangent = scatter_tok(out_part, BF16).astype(BF16)
     all_out = gather_tok(out_tangent).reshape(total_rows, channels)
 
-    back_part = sum_on_chip([lambda rows: times_t(rows, down_weight)], all_out, core)[0]
+    back_part = times_t(all_out, down_weight)
+    back_part = rows_of_core(back_part, core) + swap(rows_of_core(back_part, 1 - core), 1)
     back_hidden = jnp.sum(to_chips(back_part.astype(BF16)).astype(F32), axis=0)
     all_back = lax.all_gather(back_hidden.astype(BF16), "ch", axis=0, tiled=True).astype(F32)
     back_gate = (all_back * all_factors[:, :hidden].astype(F32)).astype(BF16)
@@ -173,7 +175,7 @@
     back_tokens = scatter_tok(in_part, BF16)
 
     local_back = local_transform(back_tokens, table, lax.Precision.HIGHEST)
-    local_back = cross_two(cross(local_back, my_index, (0, 1)), my_index, 2, 3)
+    local_back = cross_two(cross_two(local_back, my_index, 0, 1), my_index, 2, 3)
     rotated_product = local_back * root_scale * channel_signs[None, :]
     token_terms = jnp.sum(probe_signs * rotated_product, axis=0)
     pieces = gather_tok(token_terms.reshape(-1, LANES))

time: 283 us -> 279 us (0.986)
    ppermute x12 -> x14, waiting for transfers between devices: 15.8 us -> 14 us  [swap(): return lax.ppermute(value, 'ch', pairs)]
    dot_general x4 -> x3, matrix products: 8.28 us -> 7.16 us  [times_t(): lax.dot_general(rows, weight, (((1,), (1,)), ((), ())), preferred_element...]
    ppermute x12 -> x14, starting transfers between devices: 20.4 us -> 21.1 us  [swap(): return lax.ppermute(value, 'ch', pairs)]
  transfers between devices with their start and end apart: 17 -> 19, of which waited for: 13 -> 13; matrix products, arithmetic and copies ran while one was open for 8% -> 8% of each run, Pallas kernels for 0% -> 0%
where the time goes in v4:
time: 279 us; the launch traced here: 277 us
  blocking collectives  141 us (51%)
  waiting for transfers between devices  45.7 us (16%)
  starting transfers between devices  36.7 us (13%)
  matrix products  19 us (7%)
  between operations  14.7 us (5%)
  other arithmetic  13.5 us (5%)
  local copies, waits for them, and re-layouts  6.1 us (2%)
    all_to_all x2, blocking collectives, to_chips(): lax.all_to_all(blocks, 'ch', 0, 0, tiled=True, axis_index_groups=chip_gro...  56.4 us
    all_to_all x2, blocking collectives, scatter_tok(): arrived = lax.all_to_all(blocks, 'tok', 0, 0, tiled=True)  34.3 us
    all_to_all x3, waiting for transfers between devices, gather_tok(): return lax.all_to_all(copies, 'tok', 0, 0, tiled=True)  26.3 us
    ppermute x14, starting transfers between devices, swap(): return lax.ppermute(value, 'ch', pairs)  21.1 us
    all_gather x1, blocking collectives, on_device(): lax.all_gather(hidden_tan, 'ch', axis=0, tiled=True)  20.9 us
    all_gather x1, blocking collectives, on_device(): lax.all_gather(back_hidden.astype(BF16), 'ch', axis=0, tiled=True)  18.8 us
    all_to_all x3, starting transfers between devices, gather_tok(): return lax.all_to_all(copies, 'tok', 0, 0, tiled=True)  15.5 us
    ppermute x14, waiting for transfers between devices, swap(): return lax.ppermute(value, 'ch', pairs)  14 us
  transfers between devices with their start and end apart: 19, of which 13 were waited for; matrix products, arithmetic and copies ran while one was open for 8% of the time, Pallas kernels for 0%

profile of v4, /device:TPU:32, one launch (start us, length us, event | category | flops | bytes accessed | tf_op | source)
XLA Modules:
  0.0 276.6 jit_solution(11184041954427151913)
XLA Ops:
  11.9 7.0 %all-to-all-start = ((bf16[16,16,1024]{2,1,0:T(8,128)(2,1)}), bf16[16,16,1024]{2,1,0:T(8,128)(2,1)}, u32[]{:S(2)}, u32[]{:S(2)}) async-start(bf16[16,16,1024]{2,1,0:T(8,128)(2,1)} %broadcast_in_dim.62), calls=%async_computation | async-start | bytes 1048576 | tf_op jit(solution)/shard_map/all_to_all | solution.py:65
  19.8 3.4 %collective-permute-start.3 = (bf16[16,1024]{1,0:T(8,128)(2,1)S(1)}, bf16[16,1024]{1,0:T(8,128)(2,1)S(1)}, u32[]{:S(2)}, u32[]{:S(2)}) collective-permute-start(bf16[16,1024]{1,0:T(8,128)(2,1)S(1)} %add_add_fusion.1), channel_id=1, source_target_pairs={{0,4},{1,5},{2,6},{3,7},{4,0},{5,1},{6,2},{7,3},{8,12},{9,13},{10,... | collective-permute-start | bytes 98312 | tf_op jit(solution)/shard_map/ppermute | solution.py:25
  25.1 5.6 %all-to-all-done = bf16[16,16,1024]{2,1,0:T(8,128)(2,1)} async-done(((bf16[16,16,1024]{2,1,0:T(8,128)(2,1)}), bf16[16,16,1024]{2,1,0:T(8,128)(2,1)}, u32[]{:S(2)}, u32[]{:S(2)}) %all-to-all-start) | async-done | bytes 524320 | tf_op jit(solution)/shard_map/all_to_all | solution.py:65
  30.7 6.3 %collective-permute-start.4 = (bf16[16,1024]{1,0:T(8,128)(2,1)S(1)}, bf16[16,1024]{1,0:T(8,128)(2,1)S(1)}, u32[]{:S(2)}, u32[]{:S(2)}) collective-permute-start(bf16[16,1024]{1,0:T(8,128)(2,1)S(1)} %multiply_add_fusion.1), channel_id=1, source_target_pairs={{0,8},{1,9},{2,10},{3,11},{4,12},{5,13},{6,14},{7,15},{8,0},{9,1},... | collective-permute-start | bytes 98312 | tf_op jit(solution)/shard_map/ppermute | solution.py:25
  37.0 3.2 %convolution_bitcast_fusion = f32[256,1,1664]{2,0,1:T(8,128)S(1)} fusion(bf16[256,1024]{1,0:T(8,128)(2,1)} %bitcast, bf16[1024,1664]{1,0:T(8,128)(2,1)} %param.11), kind=kOutput, calls=%fused_computation.3 | convolution fusion | flops 872415232 | bytes 5636096 | tf_op jit(solution)/shard_map/dot_general | solution.py:123
  40.3 2.2 convolution_bitcast_fusion.1
  46.4 4.3 %all-to-all-start.1 = ((bf16[16,16,1024]{2,1,0:T(8,128)(2,1)}), bf16[16,16,1024]{2,1,0:T(8,128)(2,1)}, u32[]{:S(2)}, u32[]{:S(2)}) async-start(bf16[16,16,1024]{2,1,0:T(8,128)(2,1)} %broadcast_in_dim.63), calls=%async_computation.2 | async-start | bytes 1048576 | tf_op jit(solution)/shard_map/all_to_all | solution.py:65
  50.6 10.5 %all-to-all-done.1 = bf16[16,16,1024]{2,1,0:T(8,128)(2,1)} async-done(((bf16[16,16,1024]{2,1,0:T(8,128)(2,1)}), bf16[16,16,1024]{2,1,0:T(8,128)(2,1)}, u32[]{:S(2)}, u32[]{:S(2)}) %all-to-all-start.1) | async-done | bytes 524320 | tf_op jit(solution)/shard_map/all_to_all | solution.py:65
  68.2 32.8 %all_to_all.40 = f16[8,16,3456]{2,1,0:T(8,128)(2,1)S(1)} all-to-all(f16[8,16,3456]{2,1,0:T(8,128)(2,1)S(1)} %bitcast.67), channel_id=1, replica_groups={{0,2,4,6,8,10,12,14},{1,3,5,7,9,11,13,15},{16,18,20,22,24,26,28,30},{17..., dimensions={0} | all-to-all | bytes 1769472 | tf_op jit(solution)/shard_map/all_to_all | solution.py:96
  102.1 5.4 %reduce-scatter.2.cloned.1.call-done = f32[16,2,1664]{2,0,1:T(8,128)} async-done(((f32[256,2,1664]{2,0,1:T(8,128)}), f32[16,2,1664]{2,0,1:T(8,128)}) %reduce-scatter.2.cloned.1.call-update) | async-done | bytes 213008 | tf_op jit(solution)/shard_map/reduce_scatter | solution.py:148
  109.2 20.9 %all_gather.9 = bf16[256,1664]{1,0:T(8,128)(2,1)S(1)} all-gather(bf16[16,1664]{1,0:T(8,128)(2,1)S(1)} %get-tuple-element.43), channel_id=1, replica_groups=mesh['tok'=16,'ch'=16] {'ch'}, dimensions={0}, use_global_device_ids=true | all-gather | bytes 905216 | tf_op jit(solution)/shard_map/all_gather | solution.py:164
  130.2 3.1 %convolution_convert_fusion = bf16[256,1024]{1,0:T(8,128)(2,1)S(1)} fusion(bf16[256,1664]{1,0:T(8,128)(2,1)S(1)} %all_gather.9, bf16[1664,1024]{1,0:T(8,128)(2,1)} %param.12), kind=kOutput, calls=%fused_computation.12 | convolution fusion | flops 872677376 | bytes 4784128 | tf_op jit(solution)/shard_map/dot_general | solution.py:123
  133.3 19.0 %all_to_all.41 = bf16[16,16,1024]{2,1,0:T(8,128)(2,1)} all-to-all(bf16[16,16,1024]{2,1,0:T(8,128)(2,1)S(1)} %bitcast.75), channel_id=1, replica_groups=mesh['tok'=16,'ch'=16] {'tok'}, dimensions={0} | all-to-all | bytes 1048576 | tf_op jit(solution)/shard_map/all_to_all | solution.py:71
  154.2 4.3 %all-to-all-start.4 = ((bf16[16,16,1024]{2,1,0:T(8,128)(2,1)}), bf16[16,16,1024]{2,1,0:T(8,128)(2,1)}, u32[]{:S(2)}, u32[]{:S(2)}) async-start(bf16[16,16,1024]{2,1,0:T(8,128)(2,1)} %broadcast_in_dim.68), calls=%async_computation.5 | async-start | bytes 1048576 | tf_op jit(solution)/shard_map/all_to_all | solution.py:65
  159.3 10.2 %all-to-all-done.4 = bf16[16,16,1024]{2,1,0:T(8,128)(2,1)} async-done(((bf16[16,16,1024]{2,1,0:T(8,128)(2,1)}), bf16[16,16,1024]{2,1,0:T(8,128)(2,1)}, u32[]{:S(2)}, u32[]{:S(2)}) %all-to-all-start.4) | async-done | bytes 524320 | tf_op jit(solution)/shard_map/all_to_all | solution.py:65
  169.4 3.3 %fusion = f32[8,2,16,1664]{3,2,1,0:T(8,128)S(1)} fusion(bf16[8,2,16,1024]{3,2,1,0:T(8,128)(2,1)} %bitcast.10, bf16[1664,1024]{1,0:T(8,128)(2,1)} %param.12), kind=kOutput, calls=%fused_computation.1 | convolution fusion | flops 872415232 | bytes 5636096 | tf_op jit(solution)/shard_map/dot_general | solution.py:127
  172.9 2.4 collective-permute-done.7
  175.4 23.7 %all_to_all.42 = bf16[8,16,1664]{2,1,0:T(8,128)(2,1)} all-to-all(bf16[8,16,1664]{2,1,0:T(8,128)(2,1)S(1)} %bitcast.72), channel_id=1, replica_groups={{0,2,4,6,8,10,12,14},{1,3,5,7,9,11,13,15},{16,18,20,22,24,26,28,30},{17..., dimensions={0} | all-to-all | bytes 851968 | tf_op jit(solution)/shard_map/all_to_all | solution.py:96
  200.1 18.8 %all_gather.10 = bf16[256,1664]{1,0:T(8,128)(2,1)} all-gather(bf16[16,1664]{1,0:T(8,128)(2,1)S(1)} %reduce_sum.92), channel_id=1, replica_groups=mesh['tok'=16,'ch'=16] {'ch'}, dimensions={0}, use_global_device_ids=true | all-gather | bytes 905216 | tf_op jit(solution)/shard_map/all_gather | solution.py:171
  218.9 2.7 fusion.6
  223.4 15.3 %all_to_all.43 = bf16[16,16,1024]{2,1,0:T(8,128)(2,1)S(1)} all-to-all(bf16[16,16,1024]{2,1,0:T(8,128)(2,1)S(1)} %bitcast.74), channel_id=1, replica_groups=mesh['tok'=16,'ch'=16] {'tok'}, dimensions={0} | all-to-all | bytes 1048576 | tf_op jit(solution)/shard_map/all_to_all | solution.py:71
  247.8 2.4 collective-permute-start.12
  250.2 2.7 collective-permute-start.13
  258.7 10.4 %all_to_all.44 = f32[16,8,128]{2,1,0:T(8,128)S(1)} all-to-all(f32[16,8,128]{2,1,0:T(8,128)S(1)} %broadcast_in_dim.70), channel_id=1, replica_groups=mesh['tok'=16,'ch'=16] {'tok'}, dimensions={0} | all-to-all | bytes 131072 | tf_op jit(solution)/shard_map/all_to_all | solution.py:65
  (126 shorter events, 42.3 us)
Async XLA Ops:
  7.2 33.1 %copy-start = (bf16[1024,1664]{1,0:T(8,128)(2,1)S(1)}, bf16[1024,1664]{1,0:T(8,128)(2,1)}, u32[]{:S(2)}) copy-start(bf16[1024,1664]{1,0:T(8,128)(2,1)} %param.10) | copy-start | bytes 10223620
  8.2 10.7 %collective-permute-start = (bf16[16,1024]{1,0:T(8,128)(2,1)S(1)}, bf16[16,1024]{1,0:T(8,128)(2,1)S(1)}, u32[]{:S(2)}, u32[]{:S(2)}) collective-permute-start(bf16[16,1024]{1,0:T(8,128)(2,1)S(1)} %select_convert_fusion.1), channel_id=1, source_target_pairs={{0,3},{1,2},{2,1},{3,0},{4,7},{5,6},{6,5},{7,4},{8,11},{9,10},{10,... | collective-permute-start | bytes 98312 | tf_op jit(solution)/shard_map/ppermute | solution.py:25
  8.3 10.7 %collective-permute-start.1 = (bf16[16,1024]{1,0:T(8,128)(2,1)S(1)}, bf16[16,1024]{1,0:T(8,128)(2,1)S(1)}, u32[]{:S(2)}, u32[]{:S(2)}) collective-permute-start(bf16[16,1024]{1,0:T(8,128)(2,1)S(1)} %select_convert_fusion.1), channel_id=1, source_target_pairs={{0,2},{1,3},{2,0},{3,1},{4,6},{5,7},{6,4},{7,5},{8,10},{9,11},{10,... | collective-permute-start | bytes 98312 | tf_op jit(solution)/shard_map/ppermute | solution.py:25
  10.2 8.7 %collective-permute-start.2 = (bf16[16,1024]{1,0:T(8,128)(2,1)S(1)}, bf16[16,1024]{1,0:T(8,128)(2,1)S(1)}, u32[]{:S(2)}, u32[]{:S(2)}) collective-permute-start(bf16[16,1024]{1,0:T(8,128)(2,1)S(1)} %select_convert_fusion.1), channel_id=1, source_target_pairs={{0,1},{1,0},{2,3},{3,2},{4,5},{5,4},{6,7},{7,6},{8,9},{9,8},{10,11... | collective-permute-start | bytes 98312 | tf_op jit(solution)/shard_map/ppermute | solution.py:25
  11.9 18.9 %all-to-all-start = ((bf16[16,16,1024]{2,1,0:T(8,128)(2,1)}), bf16[16,16,1024]{2,1,0:T(8,128)(2,1)}, u32[]{:S(2)}, u32[]{:S(2)}) async-start(bf16[16,16,1024]{2,1,0:T(8,128)(2,1)} %broadcast_in_dim.62), calls=%async_computation | async-start | bytes 1048576 | tf_op jit(solution)/shard_map/all_to_all | solution.py:65
  18.8 88.7 %reduce-scatter.2.cloned.1.call-start = ((), (), s32[]{:S(2)}) async-start(), calls=%async_computation.9 | async-start | bytes 3620864 | tf_op jit(solution)/shard_map/reduce_scatter | solution.py:148
  19.8 5.3 %collective-permute-start.3 = (bf16[16,1024]{1,0:T(8,128)(2,1)S(1)}, bf16[16,1024]{1,0:T(8,128)(2,1)S(1)}, u32[]{:S(2)}, u32[]{:S(2)}) collective-permute-start(bf16[16,1024]{1,0:T(8,128)(2,1)S(1)} %add_add_fusion.1), channel_id=1, source_target_pairs={{0,4},{1,5},{2,6},{3,7},{4,0},{5,1},{6,2},{7,3},{8,12},{9,13},{10,... | collective-permute-start | bytes 98312 | tf_op jit(solution)/shard_map/ppermute | solution.py:25
  30.7 13.7 %collective-permute-start.4 = (bf16[16,1024]{1,0:T(8,128)(2,1)S(1)}, bf16[16,1024]{1,0:T(8,128)(2,1)S(1)}, u32[]{:S(2)}, u32[]{:S(2)}) collective-permute-start(bf16[16,1024]{1,0:T(8,128)(2,1)S(1)} %multiply_add_fusion.1), channel_id=1, source_target_pairs={{0,8},{1,9},{2,10},{3,11},{4,12},{5,13},{6,14},{7,15},{8,0},{9,1},... | collective-permute-start | bytes 98312 | tf_op jit(solution)/shard_map/ppermute | solution.py:25
  46.4 14.7 %all-to-all-start.1 = ((bf16[16,16,1024]{2,1,0:T(8,128)(2,1)}), bf16[16,16,1024]{2,1,0:T(8,128)(2,1)}, u32[]{:S(2)}, u32[]{:S(2)}) async-start(bf16[16,16,1024]{2,1,0:T(8,128)(2,1)} %broadcast_in_dim.63), calls=%async_computation.2 | async-start | bytes 1048576 | tf_op jit(solution)/shard_map/all_to_all | solution.py:65
  63.0 2.5 collective-permute-start.5
  63.9 2.9 %collective-permute-start.6 = (f32[128,1664]{1,0:T(8,128)S(1)}, f32[128,1664]{1,0:T(8,128)S(1)}, u32[]{:S(2)}, u32[]{:S(2)}) collective-permute-start(f32[128,1664]{1,0:T(8,128)S(1)} %fusion.17), channel_id=1, source_target_pairs={{0,1},{1,0},{2,3},{3,2},{4,5},{5,4},{6,7},{7,6},{8,9},{9,8},{10,11... | collective-permute-start | bytes 2555912 | tf_op jit(solution)/shard_map/ppermute | solution.py:25
  130.1 28.4 %copy-start.7 = (bf16[16,1664]{1,0:T(8,128)(2,1)S(1)}, bf16[16,1664]{1,0:T(8,128)(2,1)}, u32[]{:S(2)}) copy-start(bf16[16,1664]{1,0:T(8,128)(2,1)} %get-tuple-element.42) | copy-start | bytes 159748
  130.1 28.4 %copy-start.8 = (bf16[16,1664]{1,0:T(8,128)(2,1)S(1)}, bf16[16,1664]{1,0:T(8,128)(2,1)}, u32[]{:S(2)}) copy-start(bf16[16,1664]{1,0:T(8,128)(2,1)} %get-tuple-element.44) | copy-start | bytes 159748
  154.2 15.2 %all-to-all-start.4 = ((bf16[16,16,1024]{2,1,0:T(8,128)(2,1)}), bf16[16,16,1024]{2,1,0:T(8,128)(2,1)}, u32[]{:S(2)}, u32[]{:S(2)}) async-start(bf16[16,16,1024]{2,1,0:T(8,128)(2,1)} %broadcast_in_dim.68), calls=%async_computation.5 | async-start | bytes 1048576 | tf_op jit(solution)/shard_map/all_to_all | solution.py:65
  158.5 60.4 %all-gather.2.cloned.1.call-start = ((), (), s32[]{:S(2)}) async-start(), calls=%async_computation.10 | async-start | bytes 1810432 | tf_op jit(solution)/shard_map/all_gather | solution.py:162
  172.8 2.5 collective-permute-start.7
  222.2 30.7 %copy-start.10 = (s32[1024]{0:T(1024)S(1)}, s32[1024]{0:T(1024)}, u32[]{:S(2)}) copy-start(s32[1024]{0:T(1024)} %param.9) | copy-start | bytes 12292
  222.2 34.9 %copy-start.4 = (s32[16,1024]{1,0:T(8,128)S(1)}, s32[16,1024]{1,0:T(8,128)}, u32[]{:S(2)}) copy-start(s32[16,1024]{1,0:T(8,128)} %param.8) | copy-start | bytes 196612
  239.2 2.3 collective-permute-start.10
  239.3 4.0 %collective-permute-start.8 = (f32[16,1024]{1,0:T(8,128)S(1)}, f32[16,1024]{1,0:T(8,128)}, u32[]{:S(2)}, u32[]{:S(2)}) collective-permute-start(f32[16,1024]{1,0:T(8,128)S(1)} %constant_dynamic-update-slice_fusion.24), channel_id=1, source_target_pairs={{0,3},{1,2},{2,1},{3,0},{4,7},{5,6},{6,5},{7,4},{8,11},{9,10},{10,... | collective-permute-start | bytes 196616 | tf_op jit(solution)/shard_map/ppermute | solution.py:25
  240.2 5.1 %collective-permute-start.9 = (f32[16,1024]{1,0:T(8,128)S(1)}, f32[16,1024]{1,0:T(8,128)}, u32[]{:S(2)}, u32[]{:S(2)}) collective-permute-start(f32[16,1024]{1,0:T(8,128)S(1)} %constant_dynamic-update-slice_fusion.24), channel_id=1, source_target_pairs={{0,2},{1,3},{2,0},{3,1},{4,6},{5,7},{6,4},{7,5},{8,10},{9,11},{10,... | collective-permute-start | bytes 196616 | tf_op jit(solution)/shard_map/ppermute | solution.py:25
  246.3 8.7 %collective-permute-start.11 = (f32[16,1024]{1,0:T(8,128)S(1)}, f32[16,1024]{1,0:T(8,128)}, u32[]{:S(2)}, u32[]{:S(2)}) collective-permute-start(f32[16,1024]{1,0:T(8,128)S(1)} %add_add_fusion), channel_id=1, source_target_pairs={{0,12},{1,13},{2,14},{3,15},{4,8},{5,9},{6,10},{7,11},{8,4},{9,5},... | collective-permute-start | bytes 196616 | tf_op jit(solution)/shard_map/ppermute | solution.py:25
  247.8 8.6 %collective-permute-start.12 = (f32[16,1024]{1,0:T(8,128)S(1)}, f32[16,1024]{1,0:T(8,128)}, u32[]{:S(2)}, u32[]{:S(2)}) collective-permute-start(f32[16,1024]{1,0:T(8,128)S(1)} %add_add_fusion), channel_id=1, source_target_pairs={{0,8},{1,9},{2,10},{3,11},{4,12},{5,13},{6,14},{7,15},{8,0},{9,1},... | collective-permute-start | bytes 196616 | tf_op jit(solution)/shard_map/ppermute | solution.py:25
  250.2 6.9 %collective-permute-start.13 = (f32[16,1024]{1,0:T(8,128)S(1)}, f32[16,1024]{1,0:T(8,128)}, u32[]{:S(2)}, u32[]{:S(2)}) collective-permute-start(f32[16,1024]{1,0:T(8,128)S(1)} %add_add_fusion), channel_id=1, source_target_pairs={{0,4},{1,5},{2,6},{3,7},{4,0},{5,1},{6,2},{7,3},{8,12},{9,13},{10,... | collective-permute-start | bytes 196616 | tf_op jit(solution)/shard_map/ppermute | solution.py:25
  (7 other events, 32.6 us)
Sparse Core Ops, SparseCore 0:
  44.5 62.9 reduce-scatter.1
  161.3 41.8 all-gather.1

commit v5 on v4

--- a/solution.py
+++ b/solution.py
@@ -38,10 +38,11 @@
 def cross_two(values, my_index, low, high):
     low_sign = bit_sign(my_index, low, values.dtype)
     high_sign = bit_sign(my_index, high, values.dtype)
+    from_low = swap(values, 2**low)
     both = swap(values, 2**low + 2**high)
     from_high = swap(values, 2**high)
-    from_low = swap(values, 2**low)
-    return (both + from_high * low_sign) + (from_low * high_sign + values * (low_sign * high_sign))
+    far = from_high * low_sign + values * (low_sign * high_sign)
+    return far + (from_low * high_sign + both)
 
 
 def local_transform(values, table, precision=None):

time: 279 us -> 278 us (level)
  transfers between devices with their start and end apart: 19 -> 19, of which waited for: 13 -> 12; matrix products, arithmetic and copies ran while one was open for 8% -> 8% of each run, Pallas kernels for 0% -> 0%
where the time goes in v5:
time: 278 us; the launch traced here: 277 us
  blocking collectives  142 us (51%)
  waiting for transfers between devices  45.6 us (16%)
  starting transfers between devices  36.7 us (13%)
  matrix products  19 us (7%)
  between operations  14.7 us (5%)
  other arithmetic  13.5 us (5%)
  local copies, waits for them, and re-layouts  6.1 us (2%)
    all_to_all x2, blocking collectives, to_chips(): lax.all_to_all(blocks, 'ch', 0, 0, tiled=True, axis_index_groups=chip_gro...  56.7 us
    all_to_all x2, blocking collectives, scatter_tok(): arrived = lax.all_to_all(blocks, 'tok', 0, 0, tiled=True)  34.3 us
    all_to_all x3, waiting for transfers between devices, gather_tok(): return lax.all_to_all(copies, 'tok', 0, 0, tiled=True)  26 us
    all_gather x1, blocking collectives, on_device(): lax.all_gather(hidden_tan, 'ch', axis=0, tiled=True)  21.3 us
    ppermute x14, starting transfers between devices, swap(): return lax.ppermute(value, 'ch', pairs)  21 us
    all_gather x1, blocking collectives, on_device(): lax.all_gather(back_hidden.astype(BF16), 'ch', axis=0, tiled=True)  18.8 us
    all_to_all x3, starting transfers between devices, gather_tok(): return lax.all_to_all(copies, 'tok', 0, 0, tiled=True)  15.6 us
    ppermute x14, waiting for transfers between devices, swap(): return lax.ppermute(value, 'ch', pairs)  14.4 us
  transfers between devices with their start and end apart: 19, of which 12 were waited for; matrix products, arithmetic and copies ran while one was open for 8% of the time, Pallas kernels for 0%

profile of v5, /device:TPU:32, one launch (start us, length us, event | category | flops | bytes accessed | tf_op | source)
XLA Modules:
  0.0 277.1 jit_solution(2239270092134511588)
XLA Ops:
  12.0 7.1 %all-to-all-start = ((bf16[16,16,1024]{2,1,0:T(8,128)(2,1)}), bf16[16,16,1024]{2,1,0:T(8,128)(2,1)}, u32[]{:S(2)}, u32[]{:S(2)}) async-start(bf16[16,16,1024]{2,1,0:T(8,128)(2,1)} %broadcast_in_dim.62), calls=%async_computation | async-start | bytes 1048576 | tf_op jit(solution)/shard_map/all_to_all | solution.py:66
  20.1 3.4 %collective-permute-start.3 = (bf16[16,1024]{1,0:T(8,128)(2,1)S(1)}, bf16[16,1024]{1,0:T(8,128)(2,1)S(1)}, u32[]{:S(2)}, u32[]{:S(2)}) collective-permute-start(bf16[16,1024]{1,0:T(8,128)(2,1)S(1)} %add_add_fusion.1), channel_id=1, source_target_pairs={{0,4},{1,5},{2,6},{3,7},{4,0},{5,1},{6,2},{7,3},{8,12},{9,13},{10,... | collective-permute-start | bytes 98312 | tf_op jit(solution)/shard_map/ppermute | solution.py:25
  25.4 5.5 %all-to-all-done = bf16[16,16,1024]{2,1,0:T(8,128)(2,1)} async-done(((bf16[16,16,1024]{2,1,0:T(8,128)(2,1)}), bf16[16,16,1024]{2,1,0:T(8,128)(2,1)}, u32[]{:S(2)}, u32[]{:S(2)}) %all-to-all-start) | async-done | bytes 524320 | tf_op jit(solution)/shard_map/all_to_all | solution.py:66
  30.9 6.3 %collective-permute-start.4 = (bf16[16,1024]{1,0:T(8,128)(2,1)S(1)}, bf16[16,1024]{1,0:T(8,128)(2,1)S(1)}, u32[]{:S(2)}, u32[]{:S(2)}) collective-permute-start(bf16[16,1024]{1,0:T(8,128)(2,1)S(1)} %multiply_add_fusion.1), channel_id=1, source_target_pairs={{0,8},{1,9},{2,10},{3,11},{4,12},{5,13},{6,14},{7,15},{8,0},{9,1},... | collective-permute-start | bytes 98312 | tf_op jit(solution)/shard_map/ppermute | solution.py:25
  37.2 3.2 %convolution_bitcast_fusion = f32[256,1,1664]{2,0,1:T(8,128)S(1)} fusion(bf16[256,1024]{1,0:T(8,128)(2,1)} %bitcast, bf16[1024,1664]{1,0:T(8,128)(2,1)} %param.11), kind=kOutput, calls=%fused_computation.3 | convolution fusion | flops 872415232 | bytes 5636096 | tf_op jit(solution)/shard_map/dot_general | solution.py:124
  46.5 4.3 %all-to-all-start.1 = ((bf16[16,16,1024]{2,1,0:T(8,128)(2,1)}), bf16[16,16,1024]{2,1,0:T(8,128)(2,1)}, u32[]{:S(2)}, u32[]{:S(2)}) async-start(bf16[16,16,1024]{2,1,0:T(8,128)(2,1)} %broadcast_in_dim.63), calls=%async_computation.2 | async-start | bytes 1048576 | tf_op jit(solution)/shard_map/all_to_all | solution.py:66
  50.8 10.3 %all-to-all-done.1 = bf16[16,16,1024]{2,1,0:T(8,128)(2,1)} async-done(((bf16[16,16,1024]{2,1,0:T(8,128)(2,1)}), bf16[16,16,1024]{2,1,0:T(8,128)(2,1)}, u32[]{:S(2)}, u32[]{:S(2)}) %all-to-all-start.1) | async-done | bytes 524320 | tf_op jit(solution)/shard_map/all_to_all | solution.py:66
  68.3 32.8 %all_to_all.40 = f16[8,16,3456]{2,1,0:T(8,128)(2,1)S(1)} all-to-all(f16[8,16,3456]{2,1,0:T(8,128)(2,1)S(1)} %bitcast.67), channel_id=1, replica_groups={{0,2,4,6,8,10,12,14},{1,3,5,7,9,11,13,15},{16,18,20,22,24,26,28,30},{17..., dimensions={0} | all-to-all | bytes 1769472 | tf_op jit(solution)/shard_map/all_to_all | solution.py:97
  102.1 5.2 %reduce-scatter.2.cloned.1.call-done = f32[16,2,1664]{2,0,1:T(8,128)} async-done(((f32[256,2,1664]{2,0,1:T(8,128)}), f32[16,2,1664]{2,0,1:T(8,128)}) %reduce-scatter.2.cloned.1.call-update) | async-done | bytes 213008 | tf_op jit(solution)/shard_map/reduce_scatter | solution.py:149
  109.0 21.3 %all_gather.9 = bf16[256,1664]{1,0:T(8,128)(2,1)S(1)} all-gather(bf16[16,1664]{1,0:T(8,128)(2,1)S(1)} %get-tuple-element.43), channel_id=1, replica_groups=mesh['tok'=16,'ch'=16] {'ch'}, dimensions={0}, use_global_device_ids=true | all-gather | bytes 905216 | tf_op jit(solution)/shard_map/all_gather | solution.py:165
  130.3 3.1 %convolution_convert_fusion = bf16[256,1024]{1,0:T(8,128)(2,1)S(1)} fusion(bf16[256,1664]{1,0:T(8,128)(2,1)S(1)} %all_gather.9, bf16[1664,1024]{1,0:T(8,128)(2,1)} %param.12), kind=kOutput, calls=%fused_computation.12 | convolution fusion | flops 872677376 | bytes 4784128 | tf_op jit(solution)/shard_map/dot_general | solution.py:124
  133.5 19.1 %all_to_all.41 = bf16[16,16,1024]{2,1,0:T(8,128)(2,1)} all-to-all(bf16[16,16,1024]{2,1,0:T(8,128)(2,1)S(1)} %bitcast.75), channel_id=1, replica_groups=mesh['tok'=16,'ch'=16] {'tok'}, dimensions={0} | all-to-all | bytes 1048576 | tf_op jit(solution)/shard_map/all_to_all | solution.py:72
  154.5 4.3 %all-to-all-start.4 = ((bf16[16,16,1024]{2,1,0:T(8,128)(2,1)}), bf16[16,16,1024]{2,1,0:T(8,128)(2,1)}, u32[]{:S(2)}, u32[]{:S(2)}) async-start(bf16[16,16,1024]{2,1,0:T(8,128)(2,1)} %broadcast_in_dim.68), calls=%async_computation.5 | async-start | bytes 1048576 | tf_op jit(solution)/shard_map/all_to_all | solution.py:66
  159.5 10.2 %all-to-all-done.4 = bf16[16,16,1024]{2,1,0:T(8,128)(2,1)} async-done(((bf16[16,16,1024]{2,1,0:T(8,128)(2,1)}), bf16[16,16,1024]{2,1,0:T(8,128)(2,1)}, u32[]{:S(2)}, u32[]{:S(2)}) %all-to-all-start.4) | async-done | bytes 524320 | tf_op jit(solution)/shard_map/all_to_all | solution.py:66
  169.7 3.3 %fusion = f32[8,2,16,1664]{3,2,1,0:T(8,128)S(1)} fusion(bf16[8,2,16,1024]{3,2,1,0:T(8,128)(2,1)} %bitcast.10, bf16[1664,1024]{1,0:T(8,128)(2,1)} %param.12), kind=kOutput, calls=%fused_computation.1 | convolution fusion | flops 872415232 | bytes 5636096 | tf_op jit(solution)/shard_map/dot_general | solution.py:128
  173.2 2.4 collective-permute-done.7
  175.7 23.9 %all_to_all.42 = bf16[8,16,1664]{2,1,0:T(8,128)(2,1)} all-to-all(bf16[8,16,1664]{2,1,0:T(8,128)(2,1)S(1)} %bitcast.72), channel_id=1, replica_groups={{0,2,4,6,8,10,12,14},{1,3,5,7,9,11,13,15},{16,18,20,22,24,26,28,30},{17..., dimensions={0} | all-to-all | bytes 851968 | tf_op jit(solution)/shard_map/all_to_all | solution.py:97
  200.7 18.8 %all_gather.10 = bf16[256,1664]{1,0:T(8,128)(2,1)} all-gather(bf16[16,1664]{1,0:T(8,128)(2,1)S(1)} %reduce_sum.92), channel_id=1, replica_groups=mesh['tok'=16,'ch'=16] {'ch'}, dimensions={0}, use_global_device_ids=true | all-gather | bytes 905216 | tf_op jit(solution)/shard_map/all_gather | solution.py:172
  219.5 2.7 fusion.6
  223.9 15.3 %all_to_all.43 = bf16[16,16,1024]{2,1,0:T(8,128)(2,1)S(1)} all-to-all(bf16[16,16,1024]{2,1,0:T(8,128)(2,1)S(1)} %bitcast.74), channel_id=1, replica_groups=mesh['tok'=16,'ch'=16] {'tok'}, dimensions={0} | all-to-all | bytes 1048576 | tf_op jit(solution)/shard_map/all_to_all | solution.py:72
  245.9 2.4 collective-permute-start.11
  249.8 2.7 collective-permute-start.13
  252.5 3.0 %collective-permute-done.11 = f32[16,1024]{1,0:T(8,128)} collective-permute-done((f32[16,1024]{1,0:T(8,128)S(1)}, f32[16,1024]{1,0:T(8,128)}, u32[]{:S(2)}, u32[]{:S(2)}) %collective-permute-start.11) | collective-permute-done | bytes 65568 | tf_op jit(solution)/shard_map/ppermute | solution.py:25
  259.2 10.4 %all_to_all.44 = f32[16,8,128]{2,1,0:T(8,128)S(1)} all-to-all(f32[16,8,128]{2,1,0:T(8,128)S(1)} %broadcast_in_dim.70), channel_id=1, replica_groups=mesh['tok'=16,'ch'=16] {'tok'}, dimensions={0} | all-to-all | bytes 131072 | tf_op jit(solution)/shard_map/all_to_all | solution.py:66
  (126 shorter events, 41.6 us)
Async XLA Ops:
  7.2 33.3 %copy-start = (bf16[1024,1664]{1,0:T(8,128)(2,1)S(1)}, bf16[1024,1664]{1,0:T(8,128)(2,1)}, u32[]{:S(2)}) copy-start(bf16[1024,1664]{1,0:T(8,128)(2,1)} %param.10) | copy-start | bytes 10223620
  8.2 11.0 %collective-permute-start = (bf16[16,1024]{1,0:T(8,128)(2,1)S(1)}, bf16[16,1024]{1,0:T(8,128)(2,1)S(1)}, u32[]{:S(2)}, u32[]{:S(2)}) collective-permute-start(bf16[16,1024]{1,0:T(8,128)(2,1)S(1)} %select_convert_fusion.1), channel_id=1, source_target_pairs={{0,2},{1,3},{2,0},{3,1},{4,6},{5,7},{6,4},{7,5},{8,10},{9,11},{10,... | collective-permute-start | bytes 98312 | tf_op jit(solution)/shard_map/ppermute | solution.py:25
  10.1 9.1 %collective-permute-start.1 = (bf16[16,1024]{1,0:T(8,128)(2,1)S(1)}, bf16[16,1024]{1,0:T(8,128)(2,1)S(1)}, u32[]{:S(2)}, u32[]{:S(2)}) collective-permute-start(bf16[16,1024]{1,0:T(8,128)(2,1)S(1)} %select_convert_fusion.1), channel_id=1, source_target_pairs={{0,1},{1,0},{2,3},{3,2},{4,5},{5,4},{6,7},{7,6},{8,9},{9,8},{10,11... | collective-permute-start | bytes 98312 | tf_op jit(solution)/shard_map/ppermute | solution.py:25
  10.1 9.1 %collective-permute-start.2 = (bf16[16,1024]{1,0:T(8,128)(2,1)S(1)}, bf16[16,1024]{1,0:T(8,128)(2,1)S(1)}, u32[]{:S(2)}, u32[]{:S(2)}) collective-permute-start(bf16[16,1024]{1,0:T(8,128)(2,1)S(1)} %select_convert_fusion.1), channel_id=1, source_target_pairs={{0,3},{1,2},{2,1},{3,0},{4,7},{5,6},{6,5},{7,4},{8,11},{9,10},{10,... | collective-permute-start | bytes 98312 | tf_op jit(solution)/shard_map/ppermute | solution.py:25
  12.0 18.8 %all-to-all-start = ((bf16[16,16,1024]{2,1,0:T(8,128)(2,1)}), bf16[16,16,1024]{2,1,0:T(8,128)(2,1)}, u32[]{:S(2)}, u32[]{:S(2)}) async-start(bf16[16,16,1024]{2,1,0:T(8,128)(2,1)} %broadcast_in_dim.62), calls=%async_computation | async-start | bytes 1048576 | tf_op jit(solution)/shard_map/all_to_all | solution.py:66
  19.1 88.1 %reduce-scatter.2.cloned.1.call-start = ((), (), s32[]{:S(2)}) async-start(), calls=%async_computation.9 | async-start | bytes 3620864 | tf_op jit(solution)/shard_map/reduce_scatter | solution.py:149
  20.1 5.3 %collective-permute-start.3 = (bf16[16,1024]{1,0:T(8,128)(2,1)S(1)}, bf16[16,1024]{1,0:T(8,128)(2,1)S(1)}, u32[]{:S(2)}, u32[]{:S(2)}) collective-permute-start(bf16[16,1024]{1,0:T(8,128)(2,1)S(1)} %add_add_fusion.1), channel_id=1, source_target_pairs={{0,4},{1,5},{2,6},{3,7},{4,0},{5,1},{6,2},{7,3},{8,12},{9,13},{10,... | collective-permute-start | bytes 98312 | tf_op jit(solution)/shard_map/ppermute | solution.py:25
  30.9 13.7 %collective-permute-start.4 = (bf16[16,1024]{1,0:T(8,128)(2,1)S(1)}, bf16[16,1024]{1,0:T(8,128)(2,1)S(1)}, u32[]{:S(2)}, u32[]{:S(2)}) collective-permute-start(bf16[16,1024]{1,0:T(8,128)(2,1)S(1)} %multiply_add_fusion.1), channel_id=1, source_target_pairs={{0,8},{1,9},{2,10},{3,11},{4,12},{5,13},{6,14},{7,15},{8,0},{9,1},... | collective-permute-start | bytes 98312 | tf_op jit(solution)/shard_map/ppermute | solution.py:25
  46.5 14.6 %all-to-all-start.1 = ((bf16[16,16,1024]{2,1,0:T(8,128)(2,1)}), bf16[16,16,1024]{2,1,0:T(8,128)(2,1)}, u32[]{:S(2)}, u32[]{:S(2)}) async-start(bf16[16,16,1024]{2,1,0:T(8,128)(2,1)} %broadcast_in_dim.63), calls=%async_computation.2 | async-start | bytes 1048576 | tf_op jit(solution)/shard_map/all_to_all | solution.py:66
  63.0 2.5 collective-permute-start.5
  64.0 2.9 %collective-permute-start.6 = (f32[128,1664]{1,0:T(8,128)S(1)}, f32[128,1664]{1,0:T(8,128)S(1)}, u32[]{:S(2)}, u32[]{:S(2)}) collective-permute-start(f32[128,1664]{1,0:T(8,128)S(1)} %fusion.17), channel_id=1, source_target_pairs={{0,1},{1,0},{2,3},{3,2},{4,5},{5,4},{6,7},{7,6},{8,9},{9,8},{10,11... | collective-permute-start | bytes 2555912 | tf_op jit(solution)/shard_map/ppermute | solution.py:25
  130.3 28.5 %copy-start.7 = (bf16[16,1664]{1,0:T(8,128)(2,1)S(1)}, bf16[16,1664]{1,0:T(8,128)(2,1)}, u32[]{:S(2)}) copy-start(bf16[16,1664]{1,0:T(8,128)(2,1)} %get-tuple-element.42) | copy-start | bytes 159748
  130.3 28.5 %copy-start.8 = (bf16[16,1664]{1,0:T(8,128)(2,1)S(1)}, bf16[16,1664]{1,0:T(8,128)(2,1)}, u32[]{:S(2)}) copy-start(bf16[16,1664]{1,0:T(8,128)(2,1)} %get-tuple-element.44) | copy-start | bytes 159748
  154.5 15.2 %all-to-all-start.4 = ((bf16[16,16,1024]{2,1,0:T(8,128)(2,1)}), bf16[16,16,1024]{2,1,0:T(8,128)(2,1)}, u32[]{:S(2)}, u32[]{:S(2)}) async-start(bf16[16,16,1024]{2,1,0:T(8,128)(2,1)} %broadcast_in_dim.68), calls=%async_computation.5 | async-start | bytes 1048576 | tf_op jit(solution)/shard_map/all_to_all | solution.py:66
  158.8 60.7 %all-gather.2.cloned.1.call-start = ((), (), s32[]{:S(2)}) async-start(), calls=%async_computation.10 | async-start | bytes 1810432 | tf_op jit(solution)/shard_map/all_gather | solution.py:163
  173.1 2.5 collective-permute-start.7
  222.7 29.7 %copy-start.10 = (s32[1024]{0:T(1024)S(1)}, s32[1024]{0:T(1024)}, u32[]{:S(2)}) copy-start(s32[1024]{0:T(1024)} %param.9) | copy-start | bytes 12292
  222.7 34.9 %copy-start.4 = (s32[16,1024]{1,0:T(8,128)S(1)}, s32[16,1024]{1,0:T(8,128)}, u32[]{:S(2)}) copy-start(s32[16,1024]{1,0:T(8,128)} %param.8) | copy-start | bytes 196612
  239.7 4.1 %collective-permute-start.10 = (f32[16,1024]{1,0:T(8,128)S(1)}, f32[16,1024]{1,0:T(8,128)}, u32[]{:S(2)}, u32[]{:S(2)}) collective-permute-start(f32[16,1024]{1,0:T(8,128)S(1)} %constant_dynamic-update-slice_fusion.24), channel_id=1, source_target_pairs={{0,3},{1,2},{2,1},{3,0},{4,7},{5,6},{6,5},{7,4},{8,11},{9,10},{10,... | collective-permute-start | bytes 196616 | tf_op jit(solution)/shard_map/ppermute | solution.py:25
  239.8 5.1 %collective-permute-start.8 = (f32[16,1024]{1,0:T(8,128)S(1)}, f32[16,1024]{1,0:T(8,128)}, u32[]{:S(2)}, u32[]{:S(2)}) collective-permute-start(f32[16,1024]{1,0:T(8,128)S(1)} %constant_dynamic-update-slice_fusion.24), channel_id=1, source_target_pairs={{0,2},{1,3},{2,0},{3,1},{4,6},{5,7},{6,4},{7,5},{8,10},{9,11},{10,... | collective-permute-start | bytes 196616 | tf_op jit(solution)/shard_map/ppermute | solution.py:25
  240.7 4.2 %collective-permute-start.9 = (f32[16,1024]{1,0:T(8,128)S(1)}, f32[16,1024]{1,0:T(8,128)}, u32[]{:S(2)}, u32[]{:S(2)}) collective-permute-start(f32[16,1024]{1,0:T(8,128)S(1)} %constant_dynamic-update-slice_fusion.24), channel_id=1, source_target_pairs={{0,1},{1,0},{2,3},{3,2},{4,5},{5,4},{6,7},{7,6},{8,9},{9,8},{10,11... | collective-permute-start | bytes 196616 | tf_op jit(solution)/shard_map/ppermute | solution.py:25
  245.9 9.6 %collective-permute-start.11 = (f32[16,1024]{1,0:T(8,128)S(1)}, f32[16,1024]{1,0:T(8,128)}, u32[]{:S(2)}, u32[]{:S(2)}) collective-permute-start(f32[16,1024]{1,0:T(8,128)S(1)} %add_add_fusion), channel_id=1, source_target_pairs={{0,8},{1,9},{2,10},{3,11},{4,12},{5,13},{6,14},{7,15},{8,0},{9,1},... | collective-permute-start | bytes 196616 | tf_op jit(solution)/shard_map/ppermute | solution.py:25
  248.3 7.1 %collective-permute-start.12 = (f32[16,1024]{1,0:T(8,128)S(1)}, f32[16,1024]{1,0:T(8,128)}, u32[]{:S(2)}, u32[]{:S(2)}) collective-permute-start(f32[16,1024]{1,0:T(8,128)S(1)} %add_add_fusion), channel_id=1, source_target_pairs={{0,4},{1,5},{2,6},{3,7},{4,0},{5,1},{6,2},{7,3},{8,12},{9,13},{10,... | collective-permute-start | bytes 196616 | tf_op jit(solution)/shard_map/ppermute | solution.py:25
  249.8 7.9 %collective-permute-start.13 = (f32[16,1024]{1,0:T(8,128)S(1)}, f32[16,1024]{1,0:T(8,128)}, u32[]{:S(2)}, u32[]{:S(2)}) collective-permute-start(f32[16,1024]{1,0:T(8,128)S(1)} %add_add_fusion), channel_id=1, source_target_pairs={{0,12},{1,13},{2,14},{3,15},{4,8},{5,9},{6,10},{7,11},{8,4},{9,5},... | collective-permute-start | bytes 196616 | tf_op jit(solution)/shard_map/ppermute | solution.py:25
  (7 other events, 33.6 us)
Sparse Core Ops, SparseCore 0:
  44.7 62.5 reduce-scatter.1
  161.6 42.0 all-gather.1
